TPU v7x, 256 devices: a whole 4x4x8 slice. The times are simulated.
256 devices in a mesh: pair: 64 (over x_hi, z, y), sigma: 4 (over x_lo, core).
Axes of the slice: x: 4 (x_hi: 2, x_lo: 2; x = x_hi * 2 + x_lo), y: 4, z: 8, core: 2. Of those that a mesh axis runs over, the one named last changes fastest.
Arguments:
- pair_density_matrices: bfloat16 [131072, 1536], P('pair'), may hold values from -16 to 16
- energy_bins: int32 [131072, 2], P('pair'), may hold values from 0 to 63
- bin_weights: float32 [2, 64], replicated, may hold values from 0.05 to 1
- coulomb: float32 [1536], replicated, may hold values from 0.5 to 4
- state_matrices: bfloat16 [1536, 2048], P(None, 'sigma'), may hold values from -6 to 6
Outputs:
- screened_states: float32 [1536, 2, 2048], P('pair', None, 'sigma')
- sigma_diag: float32 [2, 2048], P(None, 'sigma')
All inputs are finite; a program needn't handle non-finite values.
Results may differ from a plain program's by a relative error of at most 0.00035.
Values sent between devices are 32-bit elements; how exact they have to be, the bound alone decides.
No kernel may reach another device: no remote copies, remote signals or barrier semaphores. Data moves between devices by JAX's collectives and lax.ppermute only.
A program may use at most 64 MiB of HBM per device.

v0:
```python
import jax
import jax.numpy as jnp
from jax import lax
from jax.experimental import pallas as pl
from jax.experimental.pallas import tpu as pltpu
from jax.sharding import PartitionSpec as P


NX, NZ, NY = 2, 8, 4
COLUMNS = 256
QUARTERS = 4
Z_ORDER = (4, 1, 3, -1, -3, 0, 2, -2)
Z_SLICES = ((0, 1), (1, 3), (3, 5), (5, 6), (6, 7), (7, 8))
X_GROUPS = [list(range(x * NZ * NY, (x + 1) * NZ * NY)) for x in range(NX)]
Y_GROUPS = [[base + y for y in range(NY)] for base in range(0, NX * NZ * NY, NY)]


def place(position):
    return position // (NZ * NY), position // NY % NZ, position % NY


def z_perm(dz):
    moves = []
    for position in range(NX * NZ * NY):
        x, z, y = place(position)
        moves.append((position, (x * NZ + (z + dz) % NZ) * NY + y))
    return moves


def x_swap(away):
    pair_count, sigma_count = lax.axis_size("pair"), lax.axis_size("sigma")
    moves = [
        (p * sigma_count + s, (p ^ (NZ * NY)) * sigma_count + (s ^ 2))
        for p in range(pair_count)
        for s in range(sigma_count)
    ]
    return lax.ppermute(away, ("pair", "sigma"), moves)


def y_send(part, dy):
    moves = []
    for position in range(NX * NZ * NY):
        x, z, y = place(position)
        moves.append((position, (x * NZ + z) * NY + (y + dy) % NY))
    return lax.ppermute(part, "pair", moves)


def y_parts(block):
    return lax.all_to_all(block, "pair", 0, 0, axis_index_groups=Y_GROUPS, tiled=True)


def added(parts, rows=slice(None)):
    return (parts[0, rows] + parts[1, rows]) + (parts[2, rows] + parts[3, rows])


def z_send(part, dz):
    return lax.ppermute(part, "pair", z_perm(dz))


def z_sum(far, up, down, keep, above, below):
    rows = keep.shape[0]
    far, up, down = z_send(far, -2), z_send(up, 1), z_send(down, -1)
    above = z_send(above + up[rows:], 2)
    below = z_send(below + down[rows:] + far, -2)
    return keep, up, down, above, below


def z_sum_both(low, high, up, down, keep, above, below):
    rows, columns = keep.shape
    half = rows // 2
    low, high = z_send(low, -2), z_send(high, 2)
    up, down = z_send(up, 1), z_send(down, -1)

    def middle(low, high, up, down, keep, above, below, above_out, below_out, keep_out):
        above_out[:half] = above[:half] + up[rows : rows + half]
        above_out[half:] = (above[half:] + up[rows + half :]) + high[...]
        below_out[:half] = (below[:half] + down[rows : rows + half]) + low[...]
        below_out[half:] = below[half:] + down[rows + half :]
        keep_out[...] = (keep[...] + up[:rows]) + down[:rows]

    keep, above, below = (pltpu.with_memory_space_constraint(part, pltpu.HBM) for part in (keep, above, below))
    above, below, keep = on_chip(middle, [(rows, columns)] * 3)(low, high, up, down, keep, above, below)
    above, below = z_send(above, 2), z_send(below, -2)

    def last(above, below, keep, out):
        out[...] = keep[...] + (above[...] + below[...])

    return on_chip(last, [(rows, columns)])(above, below, keep)[0]


def on_chip(body, shapes):
    return pl.pallas_call(
        body,
        out_shape=[jax.ShapeDtypeStruct(shape, jnp.float32) for shape in shapes],
        compiler_params=pltpu.CompilerParams(vmem_limit_bytes=12 << 20),
    )


def halves_added(parts):
    half = parts.shape[1] // 2

    def body(parts, first, second):
        first[...] = added(parts, slice(0, half))
        second[...] = added(parts, slice(half, None))

    return on_chip(body, [(half, parts.shape[2])] * 2)(parts)


def spots():
    position = lax.axis_index("pair")
    x = position // (NZ * NY)
    return lax.axis_index("sigma") ^ (2 * x), x, (position // NY) & (NZ - 1), position & (NY - 1)


def x_added(keep, other):
    rows = keep.shape[0] // NY

    def body(keep, other, *outs):
        for k, out in enumerate(outs):
            out[...] = keep[k * rows : k * rows + rows] + other[k * rows : k * rows + rows]

    return on_chip(body, [(rows, keep.shape[1])] * NY)(keep, other)


def interleaved(keep, other, two, row_count):
    columns = keep.shape[1]

    def body(keep, other, *refs):
        two, outs = refs[:NY], refs[NY:]
        for out, (low, high) in zip(outs, Z_SLICES):
            for k in range(low, high):
                rows = slice(k * row_count, k * row_count + row_count)
                at = 2 * (k - low) * row_count
                out[at : at + row_count] = keep[rows] + other[rows]
                out[at + row_count : at + 2 * row_count] = (two[0][rows] + two[1][rows]) + (two[2][rows] + two[3][rows])

    return on_chip(body, [(2 * (high - low) * row_count, columns) for low, high in Z_SLICES])(keep, other, *two)


def screened_block(ring, keep, other, root_rows, root_columns):
    rows, columns = keep.shape

    def body(kept, up, down, above, below, keep, other, by_row, by_column, out):
        for k in range(2):
            part = slice(k * rows, k * rows + rows)
            total = ((kept[part] + up[part]) + down[part]) + (above[part] + below[part])
            span = slice(k * columns, k * columns + columns)
            out[:, span] = by_row[...] * total * by_column[:, span]
        out[:, 2 * columns :] = by_row[...] * (keep[...] + other[...]) * by_column[:, 2 * columns :]

    return on_chip(body, [(rows, 3 * columns)])(*ring, keep, other, root_rows, root_columns)[0]


def fetcher(pairs_ref, pair_ref, done):
    col_count = pair_ref.shape[2]
    quarter = spots()[0]

    def first_column(step):
        return pl.multiple_of(((quarter + step) & (QUARTERS - 1)) * col_count, 128)

    def fetch(step):
        part = pairs_ref.at[:, pl.ds(first_column(step), col_count)]
        return pltpu.make_async_copy(part, pair_ref.at[step], done.at[step])

    return first_column, fetch


def multiply(first_column, fetch, pair_ref, scaled_ref, rows_ref, waited):
    for step in range(QUARTERS):
        if step >= waited:
            fetch(step).wait()
        rows_ref[pl.ds(first_column(step), pair_ref.shape[2]), :] = lax.dot_general(
            pair_ref[step],
            scaled_ref[:, : rows_ref.shape[1]],
            (((0,), (0,)), ((), ())),
            preferred_element_type=jnp.float32,
        )


def store(streams, outs, rows_ref):
    _, x, z, own_y = spots()
    before = 0
    for k, (stream, stores) in enumerate(streams):
        for out, index, keeps, dz, y in stores:
            y = y if y >= 0 else (own_y - y) & (NY - 1)
            at = ((x if keeps else 1 - x) * NZ + ((z + dz) & (NZ - 1))) * NY + y
            row_count = rows_ref.shape[0] // (NX * NZ * NY)
            rows = pl.ds(pl.multiple_of(at * row_count, 8), row_count)
            outs[before + out][index] = rows_ref[rows, k * COLUMNS : k * COLUMNS + COLUMNS]
        before += len(stream)


def first_streams(pairs, bins, table, streams):
    pair_local, width = pairs.shape
    col_count = width // QUARTERS
    total = 2 * col_count
    now = COLUMNS * len(streams)
    shapes = [shape for stream, _ in streams for shape in stream]
    count = len(shapes)

    def body(pairs_ref, bins_hbm, table_hbm, *refs):
        later_ref, bins_ref, table_ref, pair_ref, scaled_ref, rows_ref, done, small = refs[count:]
        first_column, fetch = fetcher(pairs_ref, pair_ref, done)
        bins_copy = pltpu.make_async_copy(bins_hbm, bins_ref, small.at[0])
        table_copy = pltpu.make_async_copy(table_hbm, table_ref, small.at[1])
        bins_copy.start()
        table_copy.start()
        for step in range(QUARTERS):
            fetch(step).start()
        bins_copy.wait()
        table_copy.wait()
        index = bins_ref[...]
        upper = lax.broadcasted_iota(jnp.int32, index.shape, 0) > 0
        picked = jnp.zeros(index.shape, jnp.float32)
        for level in range(table.shape[1]):
            picked = jnp.where(index == level, jnp.where(upper, table_ref[1, level], table_ref[0, level]), picked)
        weight = picked / jnp.float32(pair_local * NX * NZ * NY)
        by_pair = jnp.transpose(jnp.concatenate([weight, jnp.zeros((6, pair_local), jnp.float32)], axis=0))
        fetch(0).wait()

        def scaled(t):
            f, column = divmod(128 * t, col_count)
            product = by_pair[:, f : f + 1] * pair_ref[0, :, column : column + 128].astype(jnp.float32)
            return product.astype(jnp.bfloat16)

        for t in range(now // 128):
            scaled_ref[:, 128 * t : 128 * t + 128] = scaled(t)
        multiply(first_column, fetch, pair_ref, scaled_ref, rows_ref, 1)
        for t in range(now // 128, total // 128):
            later_ref[:, 128 * t - now : 128 * t - now + 128] = scaled(t)
        store(streams, refs, rows_ref)

    held = [pltpu.with_memory_space_constraint(array, pltpu.HBM) for array in (pairs, bins, table)]
    outs = pl.pallas_call(
        body,
        in_specs=[pl.BlockSpec(memory_space=pltpu.HBM)] * 3,
        out_specs=[pl.BlockSpec(memory_space=pltpu.VMEM)] * (count + 1),
        out_shape=[jax.ShapeDtypeStruct(shape, jnp.float32) for shape in shapes]
        + [jax.ShapeDtypeStruct((pair_local, total - now), jnp.bfloat16)],
        scratch_shapes=[
            pltpu.VMEM(bins.shape, jnp.int32),
            pltpu.SMEM(table.shape, jnp.float32),
            pltpu.VMEM((QUARTERS, pair_local, col_count), jnp.bfloat16),
            pltpu.VMEM((pair_local, now), jnp.bfloat16),
            pltpu.VMEM((width, now), jnp.float32),
            pltpu.SemaphoreType.DMA((QUARTERS,)),
            pltpu.SemaphoreType.DMA((2,)),
        ],
        compiler_params=pltpu.CompilerParams(vmem_limit_bytes=36 << 20),
    )(*held)
    return outs[:-1], outs[-1]


def last_stream(pairs, scaled, stream):
    pair_local, width = pairs.shape
    columns = scaled.shape[1]
    shapes = stream[0]

    part = pair_local // QUARTERS

    def body(pairs_ref, scaled_ref, *refs):
        pair_ref, turned_ref, sum_ref, rows_ref, done = refs[len(shapes) :]

        def fetch(step):
            return pltpu.make_async_copy(pairs_ref.at[step * part : step * part + part], pair_ref.at[step], done.at[step])

        for step in range(QUARTERS):
            fetch(step).start()
        turned_ref[...] = jnp.transpose(scaled_ref[...])
        for step in range(QUARTERS):
            fetch(step).wait()
            product = jnp.dot(
                turned_ref[:, step * part : step * part + part], pair_ref[step], preferred_element_type=jnp.float32
            )
            if step == 0:
                sum_ref[...] = product
            elif step < QUARTERS - 1:
                sum_ref[...] += product
            else:
                rows_ref[...] = jnp.transpose(sum_ref[...] + product)
        store([stream], refs, rows_ref)

    return pl.pallas_call(
        body,
        in_specs=[pl.BlockSpec(memory_space=pltpu.HBM), pl.BlockSpec(memory_space=pltpu.VMEM)],
        out_specs=[pl.BlockSpec(shape, lambda: (0, 0)) for shape in shapes],
        out_shape=[pltpu.HBM(shape, jnp.float32) for shape in shapes],
        scratch_shapes=[
            pltpu.VMEM((QUARTERS, part, width), jnp.bfloat16),
            pltpu.VMEM((columns, pair_local), jnp.bfloat16),
            pltpu.VMEM((columns, width), jnp.float32),
            pltpu.VMEM((width, columns), jnp.float32),
            pltpu.SemaphoreType.DMA((QUARTERS,)),
        ],
        compiler_params=pltpu.CompilerParams(vmem_limit_bytes=24 << 20),
    )(pltpu.with_memory_space_constraint(pairs, pltpu.HBM), scaled)


def local(pair_density_matrices, energy_bins, bin_weights, coulomb, state_matrices):
    width = pair_density_matrices.shape[1]
    pair_count = lax.axis_size("pair")
    sigma_count = lax.axis_size("sigma")
    row_count = width // pair_count
    col_count = width // sigma_count
    pair_position = lax.axis_index("pair")
    quarter = spots()[0]
    rc, n = row_count, COLUMNS
    slots = [(y, keeps, k) for y in range(NY) for keeps in (0, 1) for k in range(NZ)]

    def block(k):
        return slice(k * rc, k * rc + rc)

    b_stores = [(0, (y, block(keeps * NZ + k)), keeps, Z_ORDER[k], y) for y, keeps, k in slots]
    c_stores = [(keeps, (block(y * NZ + k),), keeps, Z_ORDER[k], -1 - y) for y, keeps, k in slots]
    a_shapes = [(NY * NX * rc // 2, n)] * 2
    a_shapes += [((high - low) * NY * NX * rc, n) for low, high in Z_SLICES[1:]]
    a_stores = []
    for y, keeps, k in slots:
        if k == 0:
            out, row = divmod(y * NX + keeps, NY * NX // 2)
        else:
            out, (low, _) = next((j, span) for j, span in enumerate(Z_SLICES) if span[0] <= k < span[1])
            out, row = out + 1, ((k - low) * NY + y) * NX + keeps
        a_stores.append((out, (block(row),), keeps, Z_ORDER[k], y))

    (b, *c), scaled = first_streams(
        pair_density_matrices,
        energy_bins.T,
        bin_weights,
        [([(NY, NX * NZ * rc, n)], b_stores), ([(NY * NZ * rc, n)] * 2, c_stores)],
    )
    a = last_stream(pair_density_matrices, scaled, (a_shapes, a_stores))

    c = x_added(c[1], x_swap(c[0]))
    c = [c[-1]] + [y_send(c[dy - 1], dy) for dy in (1, 3, 2)]
    b = halves_added(y_parts(b))
    bc = interleaved(b[1], x_swap(b[0]), c, rc)
    bc = z_sum(*bc)
    a = z_sum_both(*a).reshape(NY, NX * rc, n)
    a = y_parts(a)
    a = added(a, slice(0, rc)), added(a, slice(rc, None))
    root = jnp.sqrt(coulomb)
    root_rows = -lax.dynamic_slice_in_dim(root, pair_position * row_count, row_count, 0)
    root_columns = lax.dynamic_slice_in_dim(root, quarter * col_count, col_count, 0)
    root_columns = jnp.concatenate([root_columns, root_columns])
    screened = screened_block(bc, a[1], x_swap(a[0]), root_rows[:, None], root_columns[None, :])
    screened = screened.reshape(row_count, -1, col_count)
    gathered = lax.all_gather(screened, "sigma")
    upper = quarter != lax.axis_index("sigma")
    parts = [jnp.where(upper, gathered[k ^ 2], gathered[k]) for k in range(sigma_count)]
    states_wide = state_matrices.astype(jnp.float32)
    applied = jnp.einsum(
        "rfc,cn->rfn", jnp.concatenate(parts, axis=2), states_wide, precision=lax.Precision.HIGHEST
    )
    own_states = lax.dynamic_slice_in_dim(states_wide, pair_position * row_count, row_count, 0)
    total = jnp.sum(own_states[:, None, :] * applied, axis=0) / jnp.float32(width)
    tile = total.reshape(8, -1)
    tile += lax.ppermute(tile, "pair", [(p, p ^ (NZ * NY)) for p in range(pair_count)])
    spread = jnp.broadcast_to(tile[None], (NZ * NY,) + tile.shape)
    total = jnp.sum(lax.all_to_all(spread, "pair", 0, 0, axis_index_groups=X_GROUPS, tiled=True), axis=0).reshape(total.shape)
    return (applied, total)


def solution(mesh):
    return jax.shard_map(
        local,
        mesh=mesh,
        in_specs=(P("pair", None), P("pair", None), P(), P(), P(None, "sigma")),
        out_specs=(P("pair", None, "sigma"), P(None, "sigma")),
        check_vma=False,
    )
```

profile of v0, /device:TPU:2, one launch (start us, length us, event | category | flops | bytes accessed | tf_op | source)
XLA Modules:
  0.0 120.2 jit_solution(7974989579038503714)
XLA Ops:
  0.6 7.7 %shard_map.68 = (f32[4,384,256]{2,1,0:T(8,128)}, f32[768,256]{1,0:T(8,128)S(1)}, f32[768,256]{1,0:T(8,128)S(1)}, bf16[2048,256]{1,0:T(8,128)(2,1)S(1)}) custom-call(bf16[2048,1536]{1,0:T(8,128)(2,1)} %pairs_ref.3, s32[2,2048]{1,0:T(2,128)} %bitcast.21, f32[2,64]{1,0:T(2,128)} %table_hbm.1), custom_call_target="tpu_custom_call" | custom-call | tf_op jit(solution)/shard_map/pallas_call | solution.py:234
  8.4 0.0 copy-start
  8.4 0.9 copy-done
  9.3 4.5 %all-to-all-start = ((f32[4,384,256]{2,1,0:T(8,128)}), f32[4,384,256]{2,1,0:T(8,128)S(1)}, u32[]{:S(2)}, u32[]{:S(2)}) async-start(f32[4,384,256]{2,1,0:T(8,128)} %get-tuple-element.28), calls=%async_computation | async-start | bytes 3145728 | tf_op jit(solution)/shard_map/all_to_all | solution.py:49
  13.8 1.5 %collective-permute-start.1 = (f32[768,256]{1,0:T(8,128)}, f32[768,256]{1,0:T(8,128)}, u32[]{:S(2)}, u32[]{:S(2)}) collective-permute-start(f32[768,256]{1,0:T(8,128)} %copy-done), channel_id=1, source_target_pairs={{0,130},{1,131},{2,128},{3,129},{4,134},{5,135},{6,132},{7,133},{8... | collective-permute-start | bytes 2359304 | tf_op jit(solution)/shard_map/ppermute | solution.py:37
  15.2 4.8 %shard_map.72 = (f32[96,256]{1,0:T(8,128)}, f32[96,256]{1,0:T(8,128)}, f32[384,256]{1,0:T(8,128)}, f32[384,256]{1,0:T(8,128)}, f32[192,256]{1,0:T(8,128)}, /*index=5*/f32[192,256]{1,0:T(8,128)}, f32[192,256]{1,0:T(8,128)}) custom-call(bf16[2048,1536]{1,0:T(8,128)(2,1)} %pairs_ref.3, bf16[2048,256]{1,0:T(8,128)(2,1)S(1)} %get-tuple-element.43.scaled_ref), custom_call_target="tpu_custom_call" | custom-call | tf_op jit(solution)/shard_map/pallas_call | solution.py:283
  20.1 0.0 copy-start.3
  20.1 2.0 %collective-permute-start.12 = (f32[384,256]{1,0:T(8,128)}, f32[384,256]{1,0:T(8,128)S(1)}, u32[]{:S(2)}, u32[]{:S(2)}) collective-permute-start(f32[384,256]{1,0:T(8,128)} %get-tuple-element.46), channel_id=1, source_target_pairs={{0,16},{4,20},{8,24},{12,28},{16,32},{20,36},{24,40},{28,44},{32,4... | collective-permute-start | bytes 1179656 | tf_op jit(solution)/shard_map/ppermute | solution.py:57
  22.1 4.0 %collective-permute-start.13 = (f32[384,256]{1,0:T(8,128)}, f32[384,256]{1,0:T(8,128)S(1)}, u32[]{:S(2)}, u32[]{:S(2)}) collective-permute-start(f32[384,256]{1,0:T(8,128)} %get-tuple-element.47), channel_id=1, source_target_pairs={{0,112},{4,116},{8,120},{12,124},{16,0},{20,4},{24,8},{28,12},{32,... | collective-permute-start | bytes 1179656 | tf_op jit(solution)/shard_map/ppermute | solution.py:57
  26.1 2.4 %collective-permute-start.10 = (f32[96,256]{1,0:T(8,128)}, f32[96,256]{1,0:T(8,128)S(1)}, u32[]{:S(2)}, u32[]{:S(2)}) collective-permute-start(f32[96,256]{1,0:T(8,128)} %get-tuple-element.44), channel_id=1, source_target_pairs={{0,96},{4,100},{8,104},{12,108},{16,112},{20,116},{24,120},{28,124... | collective-permute-start | bytes 294920 | tf_op jit(solution)/shard_map/ppermute | solution.py:57
  28.5 0.5 collective-permute-start.11
  29.0 9.4 %collective-permute-done.10.low = f32[96,256]{1,0:T(8,128)S(1)} collective-permute-done((f32[96,256]{1,0:T(8,128)}, f32[96,256]{1,0:T(8,128)S(1)}, u32[]{:S(2)}, u32[]{:S(2)}) %collective-permute-start.10) | collective-permute-done | bytes 98336 | tf_op jit(solution)/shard_map/ppermute | solution.py:57
  38.4 0.7 collective-permute-done.11.high
  39.1 0.0 collective-permute-done.12.up
  39.1 0.0 collective-permute-done.13.down
  39.1 1.2 shard_map.73
  40.3 4.5 %collective-permute-start.14 = (f32[192,256]{1,0:T(8,128)S(1)}, f32[192,256]{1,0:T(8,128)S(1)}, u32[]{:S(2)}, u32[]{:S(2)}) collective-permute-start(f32[192,256]{1,0:T(8,128)S(1)} %get-tuple-element.51), channel_id=1, source_target_pairs={{0,32},{4,36},{8,40},{12,44},{16,48},{20,52},{24,56},{28,60},{32,6... | collective-permute-start | bytes 589832 | tf_op jit(solution)/shard_map/ppermute | solution.py:57
  44.9 0.0 collective-permute-start.15
  44.9 0.0 copy-done.3
  44.9 0.1 dynamic_slice.10
  45.0 5.6 %collective-permute-done.14.above = f32[192,256]{1,0:T(8,128)S(1)} collective-permute-done((f32[192,256]{1,0:T(8,128)S(1)}, f32[192,256]{1,0:T(8,128)S(1)}, u32[]{:S(2)}, u32[]{:S(2)}) %collective-permute-start.14) | collective-permute-done | bytes 196640 | tf_op jit(solution)/shard_map/ppermute | solution.py:57
  50.5 2.1 %collective-permute-done.15.below = f32[192,256]{1,0:T(8,128)S(1)} collective-permute-done((f32[192,256]{1,0:T(8,128)S(1)}, f32[192,256]{1,0:T(8,128)S(1)}, u32[]{:S(2)}, u32[]{:S(2)}) %collective-permute-start.15) | collective-permute-done | bytes 196640 | tf_op jit(solution)/shard_map/ppermute | solution.py:57
  52.6 0.7 shard_map.74
  53.3 0.0 collective-permute-done.1.other
  53.3 1.2 %shard_map.70 = (f32[192,256]{1,0:T(8,128)S(1)}, f32[192,256]{1,0:T(8,128)S(1)}, f32[192,256]{1,0:T(8,128)S(1)}, f32[192,256]{1,0:T(8,128)S(1)}) custom-call(f32[768,256]{1,0:T(8,128)S(1)} %get-tuple-element.31.keep, f32[768,256]{1,0:T(8,128)} %collective-permute-done.1.other), custom_call_target="tpu_custom_call" | custom-call | tf_op jit(solution)/shard_map/pallas_call | solution.py:122
  54.5 1.8 %collective-permute-start.2 = (f32[192,256]{1,0:T(8,128)S(1)}, f32[192,256]{1,0:T(8,128)S(1)}, u32[]{:S(2)}, u32[]{:S(2)}) collective-permute-start(f32[192,256]{1,0:T(8,128)S(1)} %get-tuple-element.34), channel_id=1, source_target_pairs={{0,4},{4,8},{8,12},{12,0},{16,20},{20,24},{24,28},{28,16},{32,36},... | collective-permute-start | bytes 589832 | tf_op jit(solution)/shard_map/ppermute | solution.py:45
  56.4 1.7 %collective-permute-start.3 = (f32[192,256]{1,0:T(8,128)S(1)}, f32[192,256]{1,0:T(8,128)S(1)}, u32[]{:S(2)}, u32[]{:S(2)}) collective-permute-start(f32[192,256]{1,0:T(8,128)S(1)} %get-tuple-element.35), channel_id=1, source_target_pairs={{0,12},{4,0},{8,4},{12,8},{16,28},{20,16},{24,20},{28,24},{32,44},... | collective-permute-start | bytes 589832 | tf_op jit(solution)/shard_map/ppermute | solution.py:45
  58.0 1.9 %collective-permute-start.4 = (f32[192,256]{1,0:T(8,128)S(1)}, f32[192,256]{1,0:T(8,128)S(1)}, u32[]{:S(2)}, u32[]{:S(2)}) collective-permute-start(f32[192,256]{1,0:T(8,128)S(1)} %get-tuple-element.36), channel_id=1, source_target_pairs={{0,8},{4,12},{8,0},{12,4},{16,24},{20,28},{24,16},{28,20},{32,40},... | collective-permute-start | bytes 589832 | tf_op jit(solution)/shard_map/ppermute | solution.py:45
  59.9 0.0 all-to-all-done.parts
  59.9 3.4 %all-to-all-start.1 = ((f32[4,48,256]{2,1,0:T(8,128)}), f32[4,48,256]{2,1,0:T(8,128)S(1)}, u32[]{:S(2)}, u32[]{:S(2)}) async-start(f32[4,48,256]{2,1,0:T(8,128)} %bitcast.1), calls=%async_computation.1 | async-start | bytes 393216 | tf_op jit(solution)/shard_map/all_to_all | solution.py:49
  63.3 0.1 shard_map.69
  63.4 0.6 collective-permute-start
  64.0 1.4 %dynamic-slice_convert_fusion = f32[24,512]{1,0:T(8,128)} fusion(bf16[1536,512]{1,0:T(8,128)(2,1)} %param.9, s32[]{:T(128)S(6)} %select_n.46), kind=kLoop, calls=%fused_computation.17 | loop fusion | flops 12288 | bytes 73732 | tf_op jit(solution)/shard_map/convert_element_type | solution.py:351
  65.4 0.0 collective-permute-done.2.refs_1_
  65.4 0.0 collective-permute-done.3.refs_2_
  65.4 0.9 collective-permute-done.4.refs_3_
  66.3 2.9 %collective-permute-done.other = f32[192,256]{1,0:T(8,128)S(1)} collective-permute-done((f32[192,256]{1,0:T(8,128)S(1)}, f32[192,256]{1,0:T(8,128)S(1)}, u32[]{:S(2)}, u32[]{:S(2)}) %collective-permute-start) | collective-permute-done | bytes 196640 | tf_op jit(solution)/shard_map/ppermute | solution.py:37
  69.1 0.1 shard_map.71
  69.2 0.0 copy-start.1
  69.2 0.4 collective-permute-start.6
  69.6 2.9 %collective-permute-start.8 = (f32[48,256]{1,0:T(8,128)S(1)}, f32[48,256]{1,0:T(8,128)S(1)}, u32[]{:S(2)}, u32[]{:S(2)}) collective-permute-start(f32[48,256]{1,0:T(8,128)S(1)} %get-tuple-element.42), channel_id=1, source_target_pairs={{0,96},{4,100},{8,104},{12,108},{16,112},{20,116},{24,120},{28,124... | collective-permute-start | bytes 147464 | tf_op jit(solution)/shard_map/ppermute | solution.py:57
  72.5 0.0 all-to-all-done.1
  72.5 0.6 collective-permute-start.16
  73.2 1.2 %collective-permute-start.5 = (f32[96,256]{1,0:T(8,128)S(1)}, f32[96,256]{1,0:T(8,128)S(1)}, u32[]{:S(2)}, u32[]{:S(2)}) collective-permute-start(f32[96,256]{1,0:T(8,128)S(1)} %get-tuple-element.38), channel_id=1, source_target_pairs={{0,16},{4,20},{8,24},{12,28},{16,32},{20,36},{24,40},{28,44},{32,4... | collective-permute-start | bytes 294920 | tf_op jit(solution)/shard_map/ppermute | solution.py:57
  74.4 0.6 collective-permute-done.8
  75.0 0.0 collective-permute-done.6.down
  75.0 4.7 %collective-permute-start.9 = (f32[48,256]{1,0:T(8,128)S(1)}, f32[48,256]{1,0:T(8,128)S(1)}, u32[]{:S(2)}, u32[]{:S(2)}) collective-permute-start(f32[48,256]{1,0:T(8,128)S(1)} %fusion.9), channel_id=1, source_target_pairs={{0,96},{4,100},{8,104},{12,108},{16,112},{20,116},{24,120},{28,124... | collective-permute-start | bytes 147464 | tf_op jit(solution)/shard_map/ppermute | solution.py:57
  79.7 0.0 collective-permute-done.5.up
  79.7 0.6 collective-permute-start.7
  80.3 0.1 negate_bitcast_fusion
  80.3 0.1 copy.13.by_row
  80.4 0.0 collective-permute-done.16.other
  80.4 2.1 %collective-permute-done.9.below = f32[48,256]{1,0:T(8,128)S(1)} collective-permute-done((f32[48,256]{1,0:T(8,128)S(1)}, f32[48,256]{1,0:T(8,128)S(1)}, u32[]{:S(2)}, u32[]{:S(2)}) %collective-permute-start.9) | collective-permute-done | bytes 49184 | tf_op jit(solution)/shard_map/ppermute | solution.py:57
  82.5 3.7 %collective-permute-done.7.above = f32[48,256]{1,0:T(8,128)S(1)} collective-permute-done((f32[48,256]{1,0:T(8,128)S(1)}, f32[48,256]{1,0:T(8,128)S(1)}, u32[]{:S(2)}, u32[]{:S(2)}) %collective-permute-start.7) | collective-permute-done | bytes 49184 | tf_op jit(solution)/shard_map/ppermute | solution.py:57
  86.3 0.1 shard_map.75
  86.4 6.9 %all_gather.3 = f32[4,24,2,384]{3,1,2,0:T(8,128)S(1)} all-gather(f32[1,24,2,384]{3,1,2,0:T(8,128)S(1)} %copy.14), channel_id=1, replica_groups=mesh['pair'=64,'sigma'=4] {'sigma'}, dimensions={0}, use_global_device_ids=true | all-gather | bytes 368640 | tf_op jit(solution)/shard_map/all_gather | solution.py:348
  93.4 0.9 multiply_reduce_fusion
  94.3 3.3 %collective-permute-start.17 = (f32[8,128]{1,0:T(8,128)S(1)}, f32[8,128]{1,0:T(8,128)S(1)}, u32[]{:S(2)}, u32[]{:S(2)}) collective-permute-start(f32[8,128]{1,0:T(8,128)S(1)} %div.21), channel_id=1, source_target_pairs={{0,128},{4,132},{8,136},{12,140},{16,144},{20,148},{24,152},{28,15... | collective-permute-start | bytes 12296 | tf_op jit(solution)/shard_map/ppermute | solution.py:358
  97.7 1.9 %collective-permute-done.17 = f32[8,128]{1,0:T(8,128)S(1)} collective-permute-done((f32[8,128]{1,0:T(8,128)S(1)}, f32[8,128]{1,0:T(8,128)S(1)}, u32[]{:S(2)}, u32[]{:S(2)}) %collective-permute-start.17) | collective-permute-done | bytes 4128 | tf_op jit(solution)/shard_map/ppermute | solution.py:358
  99.5 0.7 broadcast_in_dim.15
  100.2 8.9 %all-to-all-start.2 = ((f32[32,8,128]{2,1,0:T(8,128)}), f32[32,8,128]{2,1,0:T(8,128)S(1)}, u32[]{:S(2)}, u32[]{:S(2)}) async-start(f32[32,8,128]{2,1,0:T(8,128)} %broadcast_in_dim.15), calls=%async_computation.2 | async-start | bytes 262144 | tf_op jit(solution)/shard_map/all_to_all | solution.py:360
  109.1 0.7 copy.15
  109.8 9.8 %all-to-all-done.2 = f32[32,8,128]{2,1,0:T(8,128)S(1)} async-done(((f32[32,8,128]{2,1,0:T(8,128)}), f32[32,8,128]{2,1,0:T(8,128)S(1)}, u32[]{:S(2)}, u32[]{:S(2)}) %all-to-all-start.2) | async-done | bytes 131104 | tf_op jit(solution)/shard_map/all_to_all | solution.py:360
  119.6 0.6 reshape.31
  (16 shorter events, 0.2 us)
Async XLA Ops:
  8.4 0.9 copy-start
  9.3 50.6 %all-to-all-start = ((f32[4,384,256]{2,1,0:T(8,128)}), f32[4,384,256]{2,1,0:T(8,128)S(1)}, u32[]{:S(2)}, u32[]{:S(2)}) async-start(f32[4,384,256]{2,1,0:T(8,128)} %get-tuple-element.28), calls=%async_computation | async-start | bytes 3145728 | tf_op jit(solution)/shard_map/all_to_all | solution.py:49
  13.8 39.6 %collective-permute-start.1 = (f32[768,256]{1,0:T(8,128)}, f32[768,256]{1,0:T(8,128)}, u32[]{:S(2)}, u32[]{:S(2)}) collective-permute-start(f32[768,256]{1,0:T(8,128)} %copy-done), channel_id=1, source_target_pairs={{0,130},{1,131},{2,128},{3,129},{4,134},{5,135},{6,132},{7,133},{8... | collective-permute-start | bytes 2359304 | tf_op jit(solution)/shard_map/ppermute | solution.py:37
  20.1 24.8 %copy-start.3 = (f32[1536]{0:T(1024)S(1)}, f32[1536]{0:T(1024)}, u32[]{:S(2)}) copy-start(f32[1536]{0:T(1024)} %param.8) | copy-start | bytes 18436
  20.1 19.0 %collective-permute-start.12 = (f32[384,256]{1,0:T(8,128)}, f32[384,256]{1,0:T(8,128)S(1)}, u32[]{:S(2)}, u32[]{:S(2)}) collective-permute-start(f32[384,256]{1,0:T(8,128)} %get-tuple-element.46), channel_id=1, source_target_pairs={{0,16},{4,20},{8,24},{12,28},{16,32},{20,36},{24,40},{28,44},{32,4... | collective-permute-start | bytes 1179656 | tf_op jit(solution)/shard_map/ppermute | solution.py:57
  22.1 17.1 %collective-permute-start.13 = (f32[384,256]{1,0:T(8,128)}, f32[384,256]{1,0:T(8,128)S(1)}, u32[]{:S(2)}, u32[]{:S(2)}) collective-permute-start(f32[384,256]{1,0:T(8,128)} %get-tuple-element.47), channel_id=1, source_target_pairs={{0,112},{4,116},{8,120},{12,124},{16,0},{20,4},{24,8},{28,12},{32,... | collective-permute-start | bytes 1179656 | tf_op jit(solution)/shard_map/ppermute | solution.py:57
  26.1 12.3 %collective-permute-start.10 = (f32[96,256]{1,0:T(8,128)}, f32[96,256]{1,0:T(8,128)S(1)}, u32[]{:S(2)}, u32[]{:S(2)}) collective-permute-start(f32[96,256]{1,0:T(8,128)} %get-tuple-element.44), channel_id=1, source_target_pairs={{0,96},{4,100},{8,104},{12,108},{16,112},{20,116},{24,120},{28,124... | collective-permute-start | bytes 294920 | tf_op jit(solution)/shard_map/ppermute | solution.py:57
  28.5 10.6 %collective-permute-start.11 = (f32[96,256]{1,0:T(8,128)}, f32[96,256]{1,0:T(8,128)S(1)}, u32[]{:S(2)}, u32[]{:S(2)}) collective-permute-start(f32[96,256]{1,0:T(8,128)} %get-tuple-element.45), channel_id=1, source_target_pairs={{0,32},{4,36},{8,40},{12,44},{16,48},{20,52},{24,56},{28,60},{32,6... | collective-permute-start | bytes 294920 | tf_op jit(solution)/shard_map/ppermute | solution.py:57
  40.3 10.2 %collective-permute-start.14 = (f32[192,256]{1,0:T(8,128)S(1)}, f32[192,256]{1,0:T(8,128)S(1)}, u32[]{:S(2)}, u32[]{:S(2)}) collective-permute-start(f32[192,256]{1,0:T(8,128)S(1)} %get-tuple-element.51), channel_id=1, source_target_pairs={{0,32},{4,36},{8,40},{12,44},{16,48},{20,52},{24,56},{28,60},{32,6... | collective-permute-start | bytes 589832 | tf_op jit(solution)/shard_map/ppermute | solution.py:57
  44.9 7.8 %collective-permute-start.15 = (f32[192,256]{1,0:T(8,128)S(1)}, f32[192,256]{1,0:T(8,128)S(1)}, u32[]{:S(2)}, u32[]{:S(2)}) collective-permute-start(f32[192,256]{1,0:T(8,128)S(1)} %get-tuple-element.52), channel_id=1, source_target_pairs={{0,96},{4,100},{8,104},{12,108},{16,112},{20,116},{24,120},{28,124... | collective-permute-start | bytes 589832 | tf_op jit(solution)/shard_map/ppermute | solution.py:57
  54.5 10.8 %collective-permute-start.2 = (f32[192,256]{1,0:T(8,128)S(1)}, f32[192,256]{1,0:T(8,128)S(1)}, u32[]{:S(2)}, u32[]{:S(2)}) collective-permute-start(f32[192,256]{1,0:T(8,128)S(1)} %get-tuple-element.34), channel_id=1, source_target_pairs={{0,4},{4,8},{8,12},{12,0},{16,20},{20,24},{24,28},{28,16},{32,36},... | collective-permute-start | bytes 589832 | tf_op jit(solution)/shard_map/ppermute | solution.py:45
  56.4 9.0 %collective-permute-start.3 = (f32[192,256]{1,0:T(8,128)S(1)}, f32[192,256]{1,0:T(8,128)S(1)}, u32[]{:S(2)}, u32[]{:S(2)}) collective-permute-start(f32[192,256]{1,0:T(8,128)S(1)} %get-tuple-element.35), channel_id=1, source_target_pairs={{0,12},{4,0},{8,4},{12,8},{16,28},{20,16},{24,20},{28,24},{32,44},... | collective-permute-start | bytes 589832 | tf_op jit(solution)/shard_map/ppermute | solution.py:45
  58.0 8.2 %collective-permute-start.4 = (f32[192,256]{1,0:T(8,128)S(1)}, f32[192,256]{1,0:T(8,128)S(1)}, u32[]{:S(2)}, u32[]{:S(2)}) collective-permute-start(f32[192,256]{1,0:T(8,128)S(1)} %get-tuple-element.36), channel_id=1, source_target_pairs={{0,8},{4,12},{8,0},{12,4},{16,24},{20,28},{24,16},{28,20},{32,40},... | collective-permute-start | bytes 589832 | tf_op jit(solution)/shard_map/ppermute | solution.py:45
  59.9 12.6 %all-to-all-start.1 = ((f32[4,48,256]{2,1,0:T(8,128)}), f32[4,48,256]{2,1,0:T(8,128)S(1)}, u32[]{:S(2)}, u32[]{:S(2)}) async-start(f32[4,48,256]{2,1,0:T(8,128)} %bitcast.1), calls=%async_computation.1 | async-start | bytes 393216 | tf_op jit(solution)/shard_map/all_to_all | solution.py:49
  63.4 5.8 %collective-permute-start = (f32[192,256]{1,0:T(8,128)S(1)}, f32[192,256]{1,0:T(8,128)S(1)}, u32[]{:S(2)}, u32[]{:S(2)}) collective-permute-start(f32[192,256]{1,0:T(8,128)S(1)} %get-tuple-element.30), channel_id=1, source_target_pairs={{0,130},{1,131},{2,128},{3,129},{4,134},{5,135},{6,132},{7,133},{8... | collective-permute-start | bytes 589832 | tf_op jit(solution)/shard_map/ppermute | solution.py:37
  69.1 24.3 %copy-start.2 = (f32[24,512]{1,0:T(8,128)S(1)}, f32[24,512]{1,0:T(8,128)}, u32[]{:S(2)}) copy-start(f32[24,512]{1,0:T(8,128)} %dynamic-slice_convert_fusion) | copy-start | bytes 147460
  69.2 24.2 %copy-start.1 = (bf16[1536,512]{1,0:T(8,128)(2,1)S(1)}, bf16[1536,512]{1,0:T(8,128)(2,1)}, u32[]{:S(2)}) copy-start(bf16[1536,512]{1,0:T(8,128)(2,1)} %param.9) | copy-start | bytes 4718596
  69.2 5.8 %collective-permute-start.6 = (f32[96,256]{1,0:T(8,128)S(1)}, f32[96,256]{1,0:T(8,128)S(1)}, u32[]{:S(2)}, u32[]{:S(2)}) collective-permute-start(f32[96,256]{1,0:T(8,128)S(1)} %get-tuple-element.39), channel_id=1, source_target_pairs={{0,112},{4,116},{8,120},{12,124},{16,0},{20,4},{24,8},{28,12},{32,... | collective-permute-start | bytes 294920 | tf_op jit(solution)/shard_map/ppermute | solution.py:57
  69.6 5.4 %collective-permute-start.8 = (f32[48,256]{1,0:T(8,128)S(1)}, f32[48,256]{1,0:T(8,128)S(1)}, u32[]{:S(2)}, u32[]{:S(2)}) collective-permute-start(f32[48,256]{1,0:T(8,128)S(1)} %get-tuple-element.42), channel_id=1, source_target_pairs={{0,96},{4,100},{8,104},{12,108},{16,112},{20,116},{24,120},{28,124... | collective-permute-start | bytes 147464 | tf_op jit(solution)/shard_map/ppermute | solution.py:57
  72.5 7.9 %collective-permute-start.16 = (f32[24,256]{1,0:T(8,128)S(1)}, f32[24,256]{1,0:T(8,128)S(1)}, u32[]{:S(2)}, u32[]{:S(2)}) collective-permute-start(f32[24,256]{1,0:T(8,128)S(1)} %get-tuple-element.64), channel_id=1, source_target_pairs={{0,130},{1,131},{2,128},{3,129},{4,134},{5,135},{6,132},{7,133},{8... | collective-permute-start | bytes 73736 | tf_op jit(solution)/shard_map/ppermute | solution.py:37
  73.2 6.5 %collective-permute-start.5 = (f32[96,256]{1,0:T(8,128)S(1)}, f32[96,256]{1,0:T(8,128)S(1)}, u32[]{:S(2)}, u32[]{:S(2)}) collective-permute-start(f32[96,256]{1,0:T(8,128)S(1)} %get-tuple-element.38), channel_id=1, source_target_pairs={{0,16},{4,20},{8,24},{12,28},{16,32},{20,36},{24,40},{28,44},{32,4... | collective-permute-start | bytes 294920 | tf_op jit(solution)/shard_map/ppermute | solution.py:57
  75.0 7.5 %collective-permute-start.9 = (f32[48,256]{1,0:T(8,128)S(1)}, f32[48,256]{1,0:T(8,128)S(1)}, u32[]{:S(2)}, u32[]{:S(2)}) collective-permute-start(f32[48,256]{1,0:T(8,128)S(1)} %fusion.9), channel_id=1, source_target_pairs={{0,96},{4,100},{8,104},{12,108},{16,112},{20,116},{24,120},{28,124... | collective-permute-start | bytes 147464 | tf_op jit(solution)/shard_map/ppermute | solution.py:57
  79.7 6.6 %collective-permute-start.7 = (f32[48,256]{1,0:T(8,128)S(1)}, f32[48,256]{1,0:T(8,128)S(1)}, u32[]{:S(2)}, u32[]{:S(2)}) collective-permute-start(f32[48,256]{1,0:T(8,128)S(1)} %slice_add_fusion.1), channel_id=1, source_target_pairs={{0,32},{4,36},{8,40},{12,44},{16,48},{20,52},{24,56},{28,60},{32,6... | collective-permute-start | bytes 147464 | tf_op jit(solution)/shard_map/ppermute | solution.py:57
  94.3 5.2 %collective-permute-start.17 = (f32[8,128]{1,0:T(8,128)S(1)}, f32[8,128]{1,0:T(8,128)S(1)}, u32[]{:S(2)}, u32[]{:S(2)}) collective-permute-start(f32[8,128]{1,0:T(8,128)S(1)} %div.21), channel_id=1, source_target_pairs={{0,128},{4,132},{8,136},{12,140},{16,144},{20,148},{24,152},{28,15... | collective-permute-start | bytes 12296 | tf_op jit(solution)/shard_map/ppermute | solution.py:358
  100.2 19.4 %all-to-all-start.2 = ((f32[32,8,128]{2,1,0:T(8,128)}), f32[32,8,128]{2,1,0:T(8,128)S(1)}, u32[]{:S(2)}, u32[]{:S(2)}) async-start(f32[32,8,128]{2,1,0:T(8,128)} %broadcast_in_dim.15), calls=%async_computation.2 | async-start | bytes 262144 | tf_op jit(solution)/shard_map/all_to_all | solution.py:360
where the time goes:
time: 121 us; the launch traced here: 120 us
  starting transfers between devices  51.4 us (42%)
  waiting for transfers between devices  39.6 us (33%)
  Pallas kernels  15.9 us (13%)
  blocking collectives  6.94 us (6%)
  local copies, waits for them, and re-layouts  3.13 us (3%)
  other arithmetic  1.54 us (1%)
    ppermute x11, waiting for transfers between devices, z_send(): return lax.ppermute(part, 'pair', z_perm(dz))  24.1 us
    ppermute x11, starting transfers between devices, z_send(): return lax.ppermute(part, 'pair', z_perm(dz))  23.3 us
    all_to_all x1, waiting for transfers between devices, local(): lax.all_to_all(spread, 'pair', 0, 0, axis_index_groups=X_GROUPS, tiled=True)  9.82 us
    all_to_all x1, starting transfers between devices, local(): lax.all_to_all(spread, 'pair', 0, 0, axis_index_groups=X_GROUPS, tiled=True)  8.85 us
    all_to_all x2, starting transfers between devices, y_parts(): lax.all_to_all(block, 'pair', 0, 0, axis_index_groups=Y_GROUPS, tiled=True)  7.83 us
    pallas_call x1, Pallas kernels, first_streams(): pl.pallas_call(body, in_specs=[pl.BlockSpec(memory_space=pltpu.HBM)] * 3,...  7.74 us
    all_gather x1, blocking collectives, local(): gathered = lax.all_gather(screened, 'sigma')  6.94 us
    ppermute x3, starting transfers between devices, y_send(): return lax.ppermute(part, 'pair', moves)  5.37 us
  transfers between devices with their start and end apart: 21, of which 11 were waited for; matrix products, arithmetic and copies ran while one was open for 2% of the time, Pallas kernels for 7%

commit v1 on v0

--- a/solution.py
+++ b/solution.py
@@ -45,6 +45,10 @@
     return lax.ppermute(part, "pair", moves)
 
 
+def y_direct(blocks):
+    return [blocks[-1]] + [y_send(blocks[dy - 1], dy) for dy in (1, 3, 2)]
+
+
 def y_parts(block):
     return lax.all_to_all(block, "pair", 0, 0, axis_index_groups=Y_GROUPS, tiled=True)
 
@@ -82,10 +86,14 @@
     above, below, keep = on_chip(middle, [(rows, columns)] * 3)(low, high, up, down, keep, above, below)
     above, below = z_send(above, 2), z_send(below, -2)
 
-    def last(above, below, keep, out):
-        out[...] = keep[...] + (above[...] + below[...])
-
-    return on_chip(last, [(rows, columns)])(above, below, keep)[0]
+    part = rows // NY
+
+    def last(above, below, keep, *outs):
+        for k, out in enumerate(outs):
+            span = slice(k * part, k * part + part)
+            out[...] = keep[span] + (above[span] + below[span])
+
+    return on_chip(last, [(part, columns)] * NY)(above, below, keep)
 
 
 def on_chip(body, shapes):
@@ -321,7 +329,7 @@
         else:
             out, (low, _) = next((j, span) for j, span in enumerate(Z_SLICES) if span[0] <= k < span[1])
             out, row = out + 1, ((k - low) * NY + y) * NX + keeps
-        a_stores.append((out, (block(row),), keeps, Z_ORDER[k], y))
+        a_stores.append((out, (block(row),), keeps, Z_ORDER[k], -1 - y))
 
     (b, *c), scaled = first_streams(
         pair_density_matrices,
@@ -332,13 +340,12 @@
     a = last_stream(pair_density_matrices, scaled, (a_shapes, a_stores))
 
     c = x_added(c[1], x_swap(c[0]))
-    c = [c[-1]] + [y_send(c[dy - 1], dy) for dy in (1, 3, 2)]
+    c = y_direct(c)
     b = halves_added(y_parts(b))
     bc = interleaved(b[1], x_swap(b[0]), c, rc)
     bc = z_sum(*bc)
-    a = z_sum_both(*a).reshape(NY, NX * rc, n)
-    a = y_parts(a)
-    a = added(a, slice(0, rc)), added(a, slice(rc, None))
+    a = y_direct(z_sum_both(*a))
+    a = [(a[0][rows] + a[1][rows]) + (a[2][rows] + a[3][rows]) for rows in (slice(0, rc), slice(rc, None))]
     root = jnp.sqrt(coulomb)
     root_rows = -lax.dynamic_slice_in_dim(root, pair_position * row_count, row_count, 0)
     root_columns = lax.dynamic_slice_in_dim(root, quarter * col_count, col_count, 0)

time: 121 us -> 110 us (0.909)
  waiting for transfers between devices: 39.6 us -> 30.2 us
  starting transfers between devices: 51.4 us -> 48.8 us
    ppermute x11, waiting for transfers between devices: 24.1 us -> 15.7 us  [z_send(): return lax.ppermute(part, 'pair', z_perm(dz))]
    ppermute x3 -> x6, starting transfers between devices: 5.37 us -> 9.89 us  [y_send(): return lax.ppermute(part, 'pair', moves)]
    all_to_all x1, starting transfers between devices: 8.85 us -> 5.38 us  [local(): lax.all_to_all(spread, 'pair', 0, 0, axis_index_groups=X_GROUPS, tiled=True)]
    all_to_all x2 -> x1, starting transfers between devices: 7.83 us -> 4.47 us  [y_parts(): lax.all_to_all(block, 'pair', 0, 0, axis_index_groups=Y_GROUPS, tiled=True)]
    ppermute x3, waiting for transfers between devices: 2.87 us -> 0.01 us  [x_swap(): return lax.ppermute(away, ('pair', 'sigma'), moves)]
    ppermute x1, waiting for transfers between devices: 1.86 us -> 4.64 us  [local(): lax.ppermute(tile, 'pair', [(p, p ^ NZ * NY) for p in range(pair_count)])]
    ppermute x1, starting transfers between devices: 3.34 us -> 0.56 us  [local(): lax.ppermute(tile, 'pair', [(p, p ^ NZ * NY) for p in range(pair_count)])]
    ppermute x11, starting transfers between devices: 23.3 us -> 24.5 us  [z_send(): return lax.ppermute(part, 'pair', z_perm(dz))]
  transfers between devices with their start and end apart: 21 -> 23, of which waited for: 11 -> 6; matrix products, arithmetic and copies ran while one was open for 2% -> 2% of each run, Pallas kernels for 7% -> 8%
where the time goes in v1:
time: 110 us
  starting transfers between devices  48.8 us (44%)
  waiting for transfers between devices  30.2 us (27%)
  Pallas kernels  16.6 us (15%)
  blocking collectives  7.74 us (7%)
  local copies, waits for them, and re-layouts  3.8 us (3%)
    ppermute x11, starting transfers between devices, z_send(): return lax.ppermute(part, 'pair', z_perm(dz))  24.5 us
    ppermute x11, waiting for transfers between devices, z_send(): return lax.ppermute(part, 'pair', z_perm(dz))  15.7 us
    ppermute x6, starting transfers between devices, y_send(): return lax.ppermute(part, 'pair', moves)  9.89 us
    all_to_all x1, waiting for transfers between devices, local(): lax.all_to_all(spread, 'pair', 0, 0, axis_index_groups=X_GROUPS, tiled=True)  9.82 us
    all_gather x1, blocking collectives, local(): gathered = lax.all_gather(screened, 'sigma')  7.74 us
    pallas_call x1, Pallas kernels, first_streams(): pl.pallas_call(body, in_specs=[pl.BlockSpec(memory_space=pltpu.HBM)] * 3,...  7.73 us
    all_to_all x1, starting transfers between devices, local(): lax.all_to_all(spread, 'pair', 0, 0, axis_index_groups=X_GROUPS, tiled=True)  5.38 us
    pallas_call x1, Pallas kernels, last_stream(): pl.pallas_call(body, in_specs=[pl.BlockSpec(memory_space=pltpu.HBM), pl.B...  4.81 us
  transfers between devices with their start and end apart: 23, of which 6 were waited for; matrix products, arithmetic and copies ran while one was open for 2% of the time, Pallas kernels for 8%

profile of v1, /device:TPU:2, one launch (start us, length us, event | category | flops | bytes accessed | tf_op | source)
XLA Modules:
  0.0 109.8 jit_solution(4405208724163577245)
XLA Ops:
  0.6 7.7 %shard_map.68 = (f32[4,384,256]{2,1,0:T(8,128)}, f32[768,256]{1,0:T(8,128)S(1)}, f32[768,256]{1,0:T(8,128)S(1)}, bf16[2048,256]{1,0:T(8,128)(2,1)S(1)}) custom-call(bf16[2048,1536]{1,0:T(8,128)(2,1)} %pairs_ref.3, s32[2,2048]{1,0:T(2,128)} %bitcast.16, f32[2,64]{1,0:T(2,128)} %table_hbm.1), custom_call_target="tpu_custom_call" | custom-call | tf_op jit(solution)/shard_map/pallas_call | solution.py:242
  8.4 0.9 copy-done
  9.3 4.5 %all-to-all-start = ((f32[4,384,256]{2,1,0:T(8,128)}), f32[4,384,256]{2,1,0:T(8,128)S(1)}, u32[]{:S(2)}, u32[]{:S(2)}) async-start(f32[4,384,256]{2,1,0:T(8,128)} %get-tuple-element.32), calls=%async_computation | async-start | bytes 3145728 | tf_op jit(solution)/shard_map/all_to_all | solution.py:53
  13.7 1.5 %collective-permute-start.1 = (f32[768,256]{1,0:T(8,128)}, f32[768,256]{1,0:T(8,128)S(1)}, u32[]{:S(2)}, u32[]{:S(2)}) collective-permute-start(f32[768,256]{1,0:T(8,128)} %copy-done), channel_id=1, source_target_pairs={{0,130},{1,131},{2,128},{3,129},{4,134},{5,135},{6,132},{7,133},{8... | collective-permute-start | bytes 2359304 | tf_op jit(solution)/shard_map/ppermute | solution.py:37
  15.2 4.8 %shard_map.72 = (f32[96,256]{1,0:T(8,128)}, f32[96,256]{1,0:T(8,128)}, f32[384,256]{1,0:T(8,128)}, f32[384,256]{1,0:T(8,128)}, f32[192,256]{1,0:T(8,128)}, /*index=5*/f32[192,256]{1,0:T(8,128)}, f32[192,256]{1,0:T(8,128)}) custom-call(bf16[2048,1536]{1,0:T(8,128)(2,1)} %pairs_ref.3, bf16[2048,256]{1,0:T(8,128)(2,1)S(1)} %get-tuple-element.47.scaled_ref), custom_call_target="tpu_custom_call" | custom-call | tf_op jit(solution)/shard_map/pallas_call | solution.py:291
  20.1 2.0 %collective-permute-start.12 = (f32[384,256]{1,0:T(8,128)}, f32[384,256]{1,0:T(8,128)S(1)}, u32[]{:S(2)}, u32[]{:S(2)}) collective-permute-start(f32[384,256]{1,0:T(8,128)} %get-tuple-element.50), channel_id=1, source_target_pairs={{0,16},{4,20},{8,24},{12,28},{16,32},{20,36},{24,40},{28,44},{32,4... | collective-permute-start | bytes 1179656 | tf_op jit(solution)/shard_map/ppermute | solution.py:61
  22.1 4.0 %collective-permute-start.13 = (f32[384,256]{1,0:T(8,128)}, f32[384,256]{1,0:T(8,128)S(1)}, u32[]{:S(2)}, u32[]{:S(2)}) collective-permute-start(f32[384,256]{1,0:T(8,128)} %get-tuple-element.51), channel_id=1, source_target_pairs={{0,112},{4,116},{8,120},{12,124},{16,0},{20,4},{24,8},{28,12},{32,... | collective-permute-start | bytes 1179656 | tf_op jit(solution)/shard_map/ppermute | solution.py:61
  26.1 2.4 %collective-permute-start.10 = (f32[96,256]{1,0:T(8,128)}, f32[96,256]{1,0:T(8,128)S(1)}, u32[]{:S(2)}, u32[]{:S(2)}) collective-permute-start(f32[96,256]{1,0:T(8,128)} %get-tuple-element.48), channel_id=1, source_target_pairs={{0,96},{4,100},{8,104},{12,108},{16,112},{20,116},{24,120},{28,124... | collective-permute-start | bytes 294920 | tf_op jit(solution)/shard_map/ppermute | solution.py:61
  28.5 0.5 collective-permute-start.11
  29.0 9.4 %collective-permute-done.10.low = f32[96,256]{1,0:T(8,128)S(1)} collective-permute-done((f32[96,256]{1,0:T(8,128)}, f32[96,256]{1,0:T(8,128)S(1)}, u32[]{:S(2)}, u32[]{:S(2)}) %collective-permute-start.10) | collective-permute-done | bytes 98336 | tf_op jit(solution)/shard_map/ppermute | solution.py:61
  38.4 0.7 collective-permute-done.11.high
  39.1 0.0 collective-permute-done.12.up
  39.1 0.0 collective-permute-done.13.down
  39.1 1.9 %shard_map.73 = (f32[192,256]{1,0:T(8,128)}, f32[192,256]{1,0:T(8,128)}, f32[192,256]{1,0:T(8,128)S(1)}) custom-call(f32[96,256]{1,0:T(8,128)S(1)} %collective-permute-done.10.low, f32[96,256]{1,0:T(8,128)S(1)} %collective-permute-done.11.high, f32[384,256]{1,0:T(8,128)S(1)} %collective-permute-done.12.up, f32[384,256]{1,0:T(8,128)S(1)} %collective-permute-done.13.down, ...), custom_call_target="tpu_custom_call" | custom-call | tf_op jit(solution)/shard_map/pallas_call | solution.py:86
  41.0 4.4 %collective-permute-start.14 = (f32[192,256]{1,0:T(8,128)}, f32[192,256]{1,0:T(8,128)}, u32[]{:S(2)}, u32[]{:S(2)}) collective-permute-start(f32[192,256]{1,0:T(8,128)} %get-tuple-element.55), channel_id=1, source_target_pairs={{0,32},{4,36},{8,40},{12,44},{16,48},{20,52},{24,56},{28,60},{32,6... | collective-permute-start | bytes 589832 | tf_op jit(solution)/shard_map/ppermute | solution.py:61
  45.5 0.0 collective-permute-start.15
  45.5 0.0 collective-permute-done.1.other
  45.5 0.8 shard_map.70
  46.3 0.7 copy-done.1
  47.0 1.7 %collective-permute-start.2 = (f32[192,256]{1,0:T(8,128)}, f32[192,256]{1,0:T(8,128)S(1)}, u32[]{:S(2)}, u32[]{:S(2)}) collective-permute-start(f32[192,256]{1,0:T(8,128)} %get-tuple-element.38), channel_id=1, source_target_pairs={{0,4},{4,8},{8,12},{12,0},{16,20},{20,24},{24,28},{28,16},{32,36},... | collective-permute-start | bytes 589832 | tf_op jit(solution)/shard_map/ppermute | solution.py:45
  48.7 1.5 %collective-permute-start.3 = (f32[192,256]{1,0:T(8,128)}, f32[192,256]{1,0:T(8,128)S(1)}, u32[]{:S(2)}, u32[]{:S(2)}) collective-permute-start(f32[192,256]{1,0:T(8,128)} %get-tuple-element.39), channel_id=1, source_target_pairs={{0,12},{4,0},{8,4},{12,8},{16,28},{20,16},{24,20},{28,24},{32,44},... | collective-permute-start | bytes 589832 | tf_op jit(solution)/shard_map/ppermute | solution.py:45
  50.3 0.1 dynamic_slice.10
  50.3 2.1 %collective-permute-start.4 = (f32[192,256]{1,0:T(8,128)}, f32[192,256]{1,0:T(8,128)S(1)}, u32[]{:S(2)}, u32[]{:S(2)}) collective-permute-start(f32[192,256]{1,0:T(8,128)} %copy-done.1), channel_id=1, source_target_pairs={{0,8},{4,12},{8,0},{12,4},{16,24},{20,28},{24,16},{28,20},{32,40},... | collective-permute-start | bytes 589832 | tf_op jit(solution)/shard_map/ppermute | solution.py:45
  52.4 0.0 all-to-all-done.parts
  52.4 0.1 shard_map.69
  52.5 0.0 collective-permute-done.14.above
  52.5 0.9 collective-permute-start
  53.4 0.7 dynamic-slice_convert_fusion
  54.1 0.0 collective-permute-done.15.below
  54.1 1.1 shard_map.74
  55.2 1.1 collective-permute-start.16
  56.3 0.0 collective-permute-done.2.refs_1_
  56.3 2.3 %collective-permute-start.17 = (f32[48,256]{1,0:T(8,128)S(1)}, f32[48,256]{1,0:T(8,128)S(1)}, u32[]{:S(2)}, u32[]{:S(2)}) collective-permute-start(f32[48,256]{1,0:T(8,128)S(1)} %get-tuple-element.60), channel_id=1, source_target_pairs={{0,12},{4,0},{8,4},{12,8},{16,28},{20,16},{24,20},{28,24},{32,44},... | collective-permute-start | bytes 147464 | tf_op jit(solution)/shard_map/ppermute | solution.py:45
  58.5 0.0 collective-permute-done.3.refs_2_
  58.5 1.3 %collective-permute-start.18 = (f32[48,256]{1,0:T(8,128)S(1)}, f32[48,256]{1,0:T(8,128)S(1)}, u32[]{:S(2)}, u32[]{:S(2)}) collective-permute-start(f32[48,256]{1,0:T(8,128)S(1)} %get-tuple-element.61), channel_id=1, source_target_pairs={{0,8},{4,12},{8,0},{12,4},{16,24},{20,28},{24,16},{28,20},{32,40},... | collective-permute-start | bytes 147464 | tf_op jit(solution)/shard_map/ppermute | solution.py:45
  59.8 0.0 collective-permute-done.4.refs_3_
  59.8 0.0 collective-permute-done.other
  59.8 0.1 shard_map.71
  59.9 0.0 copy-start.2
  59.9 0.9 collective-permute-start.6
  60.8 3.7 %collective-permute-start.8 = (f32[48,256]{1,0:T(8,128)S(1)}, f32[48,256]{1,0:T(8,128)S(1)}, u32[]{:S(2)}, u32[]{:S(2)}) collective-permute-start(f32[48,256]{1,0:T(8,128)S(1)} %get-tuple-element.46), channel_id=1, source_target_pairs={{0,96},{4,100},{8,104},{12,108},{16,112},{20,116},{24,120},{28,124... | collective-permute-start | bytes 147464 | tf_op jit(solution)/shard_map/ppermute | solution.py:61
  64.5 0.0 collective-permute-done.16
  64.5 0.0 collective-permute-done.17
  64.5 0.0 collective-permute-done.18
  64.5 1.6 %collective-permute-start.19 = (f32[24,256]{1,0:T(8,128)S(1)}, f32[24,256]{1,0:T(8,128)S(1)}, u32[]{:S(2)}, u32[]{:S(2)}) collective-permute-start(f32[24,256]{1,0:T(8,128)S(1)} %get-tuple-element.72), channel_id=1, source_target_pairs={{0,130},{1,131},{2,128},{3,129},{4,134},{5,135},{6,132},{7,133},{8... | collective-permute-start | bytes 73736 | tf_op jit(solution)/shard_map/ppermute | solution.py:37
  66.1 0.3 collective-permute-start.5
  66.4 4.5 %collective-permute-start.9 = (f32[48,256]{1,0:T(8,128)S(1)}, f32[48,256]{1,0:T(8,128)S(1)}, u32[]{:S(2)}, u32[]{:S(2)}) collective-permute-start(f32[48,256]{1,0:T(8,128)S(1)} %fusion.9), channel_id=1, source_target_pairs={{0,96},{4,100},{8,104},{12,108},{16,112},{20,116},{24,120},{28,124... | collective-permute-start | bytes 147464 | tf_op jit(solution)/shard_map/ppermute | solution.py:61
  70.9 1.3 %collective-permute-done.5.up = f32[96,256]{1,0:T(8,128)S(1)} collective-permute-done((f32[96,256]{1,0:T(8,128)S(1)}, f32[96,256]{1,0:T(8,128)S(1)}, u32[]{:S(2)}, u32[]{:S(2)}) %collective-permute-start.5) | collective-permute-done | bytes 98336 | tf_op jit(solution)/shard_map/ppermute | solution.py:61
  72.2 1.7 %collective-permute-start.7 = (f32[48,256]{1,0:T(8,128)S(1)}, f32[48,256]{1,0:T(8,128)S(1)}, u32[]{:S(2)}, u32[]{:S(2)}) collective-permute-start(f32[48,256]{1,0:T(8,128)S(1)} %slice_add_fusion.1), channel_id=1, source_target_pairs={{0,32},{4,36},{8,40},{12,44},{16,48},{20,52},{24,56},{28,60},{32,6... | collective-permute-start | bytes 147464 | tf_op jit(solution)/shard_map/ppermute | solution.py:61
  73.9 0.1 negate_bitcast_fusion
  74.0 0.1 copy.13.by_row
  74.1 0.0 collective-permute-done.19.other
  74.1 0.0 collective-permute-done.9.below
  74.1 4.4 %collective-permute-done.7.above = f32[48,256]{1,0:T(8,128)S(1)} collective-permute-done((f32[48,256]{1,0:T(8,128)S(1)}, f32[48,256]{1,0:T(8,128)S(1)}, u32[]{:S(2)}, u32[]{:S(2)}) %collective-permute-start.7) | collective-permute-done | bytes 49184 | tf_op jit(solution)/shard_map/ppermute | solution.py:61
  78.5 0.1 shard_map.75
  78.6 7.7 %all_gather.3 = f32[4,24,2,384]{3,1,2,0:T(8,128)S(1)} all-gather(f32[1,24,2,384]{3,1,2,0:T(8,128)S(1)} %copy.14), channel_id=1, replica_groups=mesh['pair'=64,'sigma'=4] {'sigma'}, dimensions={0}, use_global_device_ids=true | all-gather | bytes 368640 | tf_op jit(solution)/shard_map/all_gather | solution.py:355
  86.4 0.9 multiply_reduce_fusion
  87.3 0.6 collective-permute-start.20
  87.9 4.6 %collective-permute-done.20 = f32[8,128]{1,0:T(8,128)S(1)} collective-permute-done((f32[8,128]{1,0:T(8,128)S(1)}, f32[8,128]{1,0:T(8,128)S(1)}, u32[]{:S(2)}, u32[]{:S(2)}) %collective-permute-start.20) | collective-permute-done | bytes 4128 | tf_op jit(solution)/shard_map/ppermute | solution.py:365
  92.5 0.7 broadcast_in_dim.15
  93.2 5.4 %all-to-all-start.1 = ((f32[32,8,128]{2,1,0:T(8,128)}), f32[32,8,128]{2,1,0:T(8,128)S(1)}, u32[]{:S(2)}, u32[]{:S(2)}) async-start(f32[32,8,128]{2,1,0:T(8,128)} %broadcast_in_dim.15), calls=%async_computation.1 | async-start | bytes 262144 | tf_op jit(solution)/shard_map/all_to_all | solution.py:367
  98.6 0.7 copy.15
  99.3 9.8 %all-to-all-done.1 = f32[32,8,128]{2,1,0:T(8,128)S(1)} async-done(((f32[32,8,128]{2,1,0:T(8,128)}), f32[32,8,128]{2,1,0:T(8,128)S(1)}, u32[]{:S(2)}, u32[]{:S(2)}) %all-to-all-start.1) | async-done | bytes 131104 | tf_op jit(solution)/shard_map/all_to_all | solution.py:367
  109.1 0.6 reshape.21
  (20 shorter events, 0.2 us)
Async XLA Ops:
  8.4 0.9 copy-start
  9.3 43.1 %all-to-all-start = ((f32[4,384,256]{2,1,0:T(8,128)}), f32[4,384,256]{2,1,0:T(8,128)S(1)}, u32[]{:S(2)}, u32[]{:S(2)}) async-start(f32[4,384,256]{2,1,0:T(8,128)} %get-tuple-element.32), calls=%async_computation | async-start | bytes 3145728 | tf_op jit(solution)/shard_map/all_to_all | solution.py:53
  13.7 31.7 %collective-permute-start.1 = (f32[768,256]{1,0:T(8,128)}, f32[768,256]{1,0:T(8,128)S(1)}, u32[]{:S(2)}, u32[]{:S(2)}) collective-permute-start(f32[768,256]{1,0:T(8,128)} %copy-done), channel_id=1, source_target_pairs={{0,130},{1,131},{2,128},{3,129},{4,134},{5,135},{6,132},{7,133},{8... | collective-permute-start | bytes 2359304 | tf_op jit(solution)/shard_map/ppermute | solution.py:37
  20.1 19.0 %collective-permute-start.12 = (f32[384,256]{1,0:T(8,128)}, f32[384,256]{1,0:T(8,128)S(1)}, u32[]{:S(2)}, u32[]{:S(2)}) collective-permute-start(f32[384,256]{1,0:T(8,128)} %get-tuple-element.50), channel_id=1, source_target_pairs={{0,16},{4,20},{8,24},{12,28},{16,32},{20,36},{24,40},{28,44},{32,4... | collective-permute-start | bytes 1179656 | tf_op jit(solution)/shard_map/ppermute | solution.py:61
  22.1 17.1 %collective-permute-start.13 = (f32[384,256]{1,0:T(8,128)}, f32[384,256]{1,0:T(8,128)S(1)}, u32[]{:S(2)}, u32[]{:S(2)}) collective-permute-start(f32[384,256]{1,0:T(8,128)} %get-tuple-element.51), channel_id=1, source_target_pairs={{0,112},{4,116},{8,120},{12,124},{16,0},{20,4},{24,8},{28,12},{32,... | collective-permute-start | bytes 1179656 | tf_op jit(solution)/shard_map/ppermute | solution.py:61
  26.1 12.3 %collective-permute-start.10 = (f32[96,256]{1,0:T(8,128)}, f32[96,256]{1,0:T(8,128)S(1)}, u32[]{:S(2)}, u32[]{:S(2)}) collective-permute-start(f32[96,256]{1,0:T(8,128)} %get-tuple-element.48), channel_id=1, source_target_pairs={{0,96},{4,100},{8,104},{12,108},{16,112},{20,116},{24,120},{28,124... | collective-permute-start | bytes 294920 | tf_op jit(solution)/shard_map/ppermute | solution.py:61
  28.5 10.6 %collective-permute-start.11 = (f32[96,256]{1,0:T(8,128)}, f32[96,256]{1,0:T(8,128)S(1)}, u32[]{:S(2)}, u32[]{:S(2)}) collective-permute-start(f32[96,256]{1,0:T(8,128)} %get-tuple-element.49), channel_id=1, source_target_pairs={{0,32},{4,36},{8,40},{12,44},{16,48},{20,52},{24,56},{28,60},{32,6... | collective-permute-start | bytes 294920 | tf_op jit(solution)/shard_map/ppermute | solution.py:61
  39.1 11.1 %copy-start.3 = (f32[1536]{0:T(1024)S(1)}, f32[1536]{0:T(1024)}, u32[]{:S(2)}) copy-start(f32[1536]{0:T(1024)} %param.8) | copy-start | bytes 18436
  41.0 11.4 %collective-permute-start.14 = (f32[192,256]{1,0:T(8,128)}, f32[192,256]{1,0:T(8,128)}, u32[]{:S(2)}, u32[]{:S(2)}) collective-permute-start(f32[192,256]{1,0:T(8,128)} %get-tuple-element.55), channel_id=1, source_target_pairs={{0,32},{4,36},{8,40},{12,44},{16,48},{20,52},{24,56},{28,60},{32,6... | collective-permute-start | bytes 589832 | tf_op jit(solution)/shard_map/ppermute | solution.py:61
  45.5 8.7 %collective-permute-start.15 = (f32[192,256]{1,0:T(8,128)}, f32[192,256]{1,0:T(8,128)}, u32[]{:S(2)}, u32[]{:S(2)}) collective-permute-start(f32[192,256]{1,0:T(8,128)} %get-tuple-element.56), channel_id=1, source_target_pairs={{0,96},{4,100},{8,104},{12,108},{16,112},{20,116},{24,120},{28,124... | collective-permute-start | bytes 589832 | tf_op jit(solution)/shard_map/ppermute | solution.py:61
  46.3 0.7 copy-start.1
  47.0 9.3 %collective-permute-start.2 = (f32[192,256]{1,0:T(8,128)}, f32[192,256]{1,0:T(8,128)S(1)}, u32[]{:S(2)}, u32[]{:S(2)}) collective-permute-start(f32[192,256]{1,0:T(8,128)} %get-tuple-element.38), channel_id=1, source_target_pairs={{0,4},{4,8},{8,12},{12,0},{16,20},{20,24},{24,28},{28,16},{32,36},... | collective-permute-start | bytes 589832 | tf_op jit(solution)/shard_map/ppermute | solution.py:45
  48.7 9.8 %collective-permute-start.3 = (f32[192,256]{1,0:T(8,128)}, f32[192,256]{1,0:T(8,128)S(1)}, u32[]{:S(2)}, u32[]{:S(2)}) collective-permute-start(f32[192,256]{1,0:T(8,128)} %get-tuple-element.39), channel_id=1, source_target_pairs={{0,12},{4,0},{8,4},{12,8},{16,28},{20,16},{24,20},{28,24},{32,44},... | collective-permute-start | bytes 589832 | tf_op jit(solution)/shard_map/ppermute | solution.py:45
  50.3 9.5 %collective-permute-start.4 = (f32[192,256]{1,0:T(8,128)}, f32[192,256]{1,0:T(8,128)S(1)}, u32[]{:S(2)}, u32[]{:S(2)}) collective-permute-start(f32[192,256]{1,0:T(8,128)} %copy-done.1), channel_id=1, source_target_pairs={{0,8},{4,12},{8,0},{12,4},{16,24},{20,28},{24,16},{28,20},{32,40},... | collective-permute-start | bytes 589832 | tf_op jit(solution)/shard_map/ppermute | solution.py:45
  52.5 7.3 %collective-permute-start = (f32[192,256]{1,0:T(8,128)S(1)}, f32[192,256]{1,0:T(8,128)S(1)}, u32[]{:S(2)}, u32[]{:S(2)}) collective-permute-start(f32[192,256]{1,0:T(8,128)S(1)} %get-tuple-element.34), channel_id=1, source_target_pairs={{0,130},{1,131},{2,128},{3,129},{4,134},{5,135},{6,132},{7,133},{8... | collective-permute-start | bytes 589832 | tf_op jit(solution)/shard_map/ppermute | solution.py:37
  55.2 9.3 %collective-permute-start.16 = (f32[48,256]{1,0:T(8,128)S(1)}, f32[48,256]{1,0:T(8,128)S(1)}, u32[]{:S(2)}, u32[]{:S(2)}) collective-permute-start(f32[48,256]{1,0:T(8,128)S(1)} %get-tuple-element.59), channel_id=1, source_target_pairs={{0,4},{4,8},{8,12},{12,0},{16,20},{20,24},{24,28},{28,16},{32,36},... | collective-permute-start | bytes 147464 | tf_op jit(solution)/shard_map/ppermute | solution.py:45
  56.3 8.3 %collective-permute-start.17 = (f32[48,256]{1,0:T(8,128)S(1)}, f32[48,256]{1,0:T(8,128)S(1)}, u32[]{:S(2)}, u32[]{:S(2)}) collective-permute-start(f32[48,256]{1,0:T(8,128)S(1)} %get-tuple-element.60), channel_id=1, source_target_pairs={{0,12},{4,0},{8,4},{12,8},{16,28},{20,16},{24,20},{28,24},{32,44},... | collective-permute-start | bytes 147464 | tf_op jit(solution)/shard_map/ppermute | solution.py:45
  58.5 6.0 %collective-permute-start.18 = (f32[48,256]{1,0:T(8,128)S(1)}, f32[48,256]{1,0:T(8,128)S(1)}, u32[]{:S(2)}, u32[]{:S(2)}) collective-permute-start(f32[48,256]{1,0:T(8,128)S(1)} %get-tuple-element.61), channel_id=1, source_target_pairs={{0,8},{4,12},{8,0},{12,4},{16,24},{20,28},{24,16},{28,20},{32,40},... | collective-permute-start | bytes 147464 | tf_op jit(solution)/shard_map/ppermute | solution.py:45
  59.9 26.5 %copy-start.2 = (bf16[1536,512]{1,0:T(8,128)(2,1)S(1)}, bf16[1536,512]{1,0:T(8,128)(2,1)}, u32[]{:S(2)}) copy-start(bf16[1536,512]{1,0:T(8,128)(2,1)} %param.9) | copy-start | bytes 4718596
  59.9 6.5 %collective-permute-start.6 = (f32[96,256]{1,0:T(8,128)S(1)}, f32[96,256]{1,0:T(8,128)S(1)}, u32[]{:S(2)}, u32[]{:S(2)}) collective-permute-start(f32[96,256]{1,0:T(8,128)S(1)} %get-tuple-element.43), channel_id=1, source_target_pairs={{0,112},{4,116},{8,120},{12,124},{16,0},{20,4},{24,8},{28,12},{32,... | collective-permute-start | bytes 294920 | tf_op jit(solution)/shard_map/ppermute | solution.py:61
  60.8 5.6 %collective-permute-start.8 = (f32[48,256]{1,0:T(8,128)S(1)}, f32[48,256]{1,0:T(8,128)S(1)}, u32[]{:S(2)}, u32[]{:S(2)}) collective-permute-start(f32[48,256]{1,0:T(8,128)S(1)} %get-tuple-element.46), channel_id=1, source_target_pairs={{0,96},{4,100},{8,104},{12,108},{16,112},{20,116},{24,120},{28,124... | collective-permute-start | bytes 147464 | tf_op jit(solution)/shard_map/ppermute | solution.py:61
  64.5 9.5 %collective-permute-start.19 = (f32[24,256]{1,0:T(8,128)S(1)}, f32[24,256]{1,0:T(8,128)S(1)}, u32[]{:S(2)}, u32[]{:S(2)}) collective-permute-start(f32[24,256]{1,0:T(8,128)S(1)} %get-tuple-element.72), channel_id=1, source_target_pairs={{0,130},{1,131},{2,128},{3,129},{4,134},{5,135},{6,132},{7,133},{8... | collective-permute-start | bytes 73736 | tf_op jit(solution)/shard_map/ppermute | solution.py:37
  66.1 6.1 %collective-permute-start.5 = (f32[96,256]{1,0:T(8,128)S(1)}, f32[96,256]{1,0:T(8,128)S(1)}, u32[]{:S(2)}, u32[]{:S(2)}) collective-permute-start(f32[96,256]{1,0:T(8,128)S(1)} %get-tuple-element.42), channel_id=1, source_target_pairs={{0,16},{4,20},{8,24},{12,28},{16,32},{20,36},{24,40},{28,44},{32,4... | collective-permute-start | bytes 294920 | tf_op jit(solution)/shard_map/ppermute | solution.py:61
  66.4 7.7 %collective-permute-start.9 = (f32[48,256]{1,0:T(8,128)S(1)}, f32[48,256]{1,0:T(8,128)S(1)}, u32[]{:S(2)}, u32[]{:S(2)}) collective-permute-start(f32[48,256]{1,0:T(8,128)S(1)} %fusion.9), channel_id=1, source_target_pairs={{0,96},{4,100},{8,104},{12,108},{16,112},{20,116},{24,120},{28,124... | collective-permute-start | bytes 147464 | tf_op jit(solution)/shard_map/ppermute | solution.py:61
  72.2 6.3 %collective-permute-start.7 = (f32[48,256]{1,0:T(8,128)S(1)}, f32[48,256]{1,0:T(8,128)S(1)}, u32[]{:S(2)}, u32[]{:S(2)}) collective-permute-start(f32[48,256]{1,0:T(8,128)S(1)} %slice_add_fusion.1), channel_id=1, source_target_pairs={{0,32},{4,36},{8,40},{12,44},{16,48},{20,52},{24,56},{28,60},{32,6... | collective-permute-start | bytes 147464 | tf_op jit(solution)/shard_map/ppermute | solution.py:61
  87.3 5.2 %collective-permute-start.20 = (f32[8,128]{1,0:T(8,128)S(1)}, f32[8,128]{1,0:T(8,128)S(1)}, u32[]{:S(2)}, u32[]{:S(2)}) collective-permute-start(f32[8,128]{1,0:T(8,128)S(1)} %div.21), channel_id=1, source_target_pairs={{0,128},{4,132},{8,136},{12,140},{16,144},{20,148},{24,152},{28,15... | collective-permute-start | bytes 12296 | tf_op jit(solution)/shard_map/ppermute | solution.py:365
  93.2 15.9 %all-to-all-start.1 = ((f32[32,8,128]{2,1,0:T(8,128)}), f32[32,8,128]{2,1,0:T(8,128)S(1)}, u32[]{:S(2)}, u32[]{:S(2)}) async-start(f32[32,8,128]{2,1,0:T(8,128)} %broadcast_in_dim.15), calls=%async_computation.1 | async-start | bytes 262144 | tf_op jit(solution)/shard_map/all_to_all | solution.py:367

commit v2 on v1

--- a/solution.py
+++ b/solution.py
@@ -12,7 +12,6 @@
 Z_ORDER = (4, 1, 3, -1, -3, 0, 2, -2)
 Z_SLICES = ((0, 1), (1, 3), (3, 5), (5, 6), (6, 7), (7, 8))
 X_GROUPS = [list(range(x * NZ * NY, (x + 1) * NZ * NY)) for x in range(NX)]
-Y_GROUPS = [[base + y for y in range(NY)] for base in range(0, NX * NZ * NY, NY)]
 
 
 def place(position):
@@ -49,14 +48,6 @@
     return [blocks[-1]] + [y_send(blocks[dy - 1], dy) for dy in (1, 3, 2)]
 
 
-def y_parts(block):
-    return lax.all_to_all(block, "pair", 0, 0, axis_index_groups=Y_GROUPS, tiled=True)
-
-
-def added(parts, rows=slice(None)):
-    return (parts[0, rows] + parts[1, rows]) + (parts[2, rows] + parts[3, rows])
-
-
 def z_send(part, dz):
     return lax.ppermute(part, "pair", z_perm(dz))
 
@@ -105,13 +96,14 @@
 
 
 def halves_added(parts):
-    half = parts.shape[1] // 2
-
-    def body(parts, first, second):
-        first[...] = added(parts, slice(0, half))
-        second[...] = added(parts, slice(half, None))
-
-    return on_chip(body, [(half, parts.shape[2])] * 2)(parts)
+    half, columns = parts[0].shape[0] // 2, parts[0].shape[1]
+
+    def body(one, two, three, four, *outs):
+        for k, out in enumerate(outs):
+            rows = slice(k * half, k * half + half)
+            out[...] = (one[rows] + two[rows]) + (three[rows] + four[rows])
+
+    return on_chip(body, [(half, columns)] * 2)(*parts)
 
 
 def spots():
@@ -318,7 +310,7 @@
     def block(k):
         return slice(k * rc, k * rc + rc)
 
-    b_stores = [(0, (y, block(keeps * NZ + k)), keeps, Z_ORDER[k], y) for y, keeps, k in slots]
+    b_stores = [(y, (block(keeps * NZ + k),), keeps, Z_ORDER[k], -1 - y) for y, keeps, k in slots]
     c_stores = [(keeps, (block(y * NZ + k),), keeps, Z_ORDER[k], -1 - y) for y, keeps, k in slots]
     a_shapes = [(NY * NX * rc // 2, n)] * 2
     a_shapes += [((high - low) * NY * NX * rc, n) for low, high in Z_SLICES[1:]]
@@ -331,17 +323,17 @@
             out, row = out + 1, ((k - low) * NY + y) * NX + keeps
         a_stores.append((out, (block(row),), keeps, Z_ORDER[k], -1 - y))
 
-    (b, *c), scaled = first_streams(
+    (*b, c_away, c_keep), scaled = first_streams(
         pair_density_matrices,
         energy_bins.T,
         bin_weights,
-        [([(NY, NX * NZ * rc, n)], b_stores), ([(NY * NZ * rc, n)] * 2, c_stores)],
+        [([(NX * NZ * rc, n)] * NY, b_stores), ([(NY * NZ * rc, n)] * 2, c_stores)],
     )
     a = last_stream(pair_density_matrices, scaled, (a_shapes, a_stores))
 
-    c = x_added(c[1], x_swap(c[0]))
+    c = x_added(c_keep, x_swap(c_away))
     c = y_direct(c)
-    b = halves_added(y_parts(b))
+    b = halves_added(y_direct(b))
     bc = interleaved(b[1], x_swap(b[0]), c, rc)
     bc = z_sum(*bc)
     a = y_direct(z_sum_both(*a))

time: 110 us -> 116 us (1.055)
  waiting for transfers between devices: 30.2 us -> 37.1 us
  starting transfers between devices: 48.8 us -> 53.8 us
  Pallas kernels: 16.6 us -> 12.9 us
  local copies, waits for them, and re-layouts: 3.8 us -> 2.23 us
    ppermute x6 -> x9, waiting for transfers between devices: 0.02 us -> 8.65 us  [y_send(): return lax.ppermute(part, 'pair', moves)]
    ppermute x6 -> x9, starting transfers between devices: 9.89 us -> 15.2 us  [y_send(): return lax.ppermute(part, 'pair', moves)]
    all_to_all x1 -> x0, starting transfers between devices: 4.47 us -> none  [y_parts(): lax.all_to_all(block, 'pair', 0, 0, axis_index_groups=Y_GROUPS, tiled=True)]
    all_to_all x1, starting transfers between devices: 5.38 us -> 7.55 us  [local(): lax.all_to_all(spread, 'pair', 0, 0, axis_index_groups=X_GROUPS, tiled=True)]
    ppermute x11, starting transfers between devices: 24.5 us -> 26.6 us  [z_send(): return lax.ppermute(part, 'pair', z_perm(dz))]
    unnamed x9 -> x5, local copies, waits for them, and re-layouts: 2.31 us -> 0.73 us
    ppermute x11, waiting for transfers between devices: 15.7 us -> 14.2 us  [z_send(): return lax.ppermute(part, 'pair', z_perm(dz))]
    pallas_call x1, Pallas kernels: 7.73 us -> 6.55 us  [first_streams(): pl.pallas_call(body, in_specs=[pl.BlockSpec(memory_space=pltpu.HBM)] * 3,...]
  transfers between devices with their start and end apart: 23 -> 25, of which waited for: 6 -> 10; matrix products, arithmetic and copies ran while one was open for 2% -> 2% of each run, Pallas kernels for 8% -> 1%
where the time goes in v2:
time: 116 us
  starting transfers between devices  53.8 us (46%)
  waiting for transfers between devices  37.1 us (32%)
  Pallas kernels  12.9 us (11%)
  blocking collectives  7.44 us (6%)
  local copies, waits for them, and re-layouts  2.23 us (2%)
    ppermute x11, starting transfers between devices, z_send(): return lax.ppermute(part, 'pair', z_perm(dz))  26.6 us
    ppermute x9, starting transfers between devices, y_send(): return lax.ppermute(part, 'pair', moves)  15.2 us
    ppermute x11, waiting for transfers between devices, z_send(): return lax.ppermute(part, 'pair', z_perm(dz))  14.2 us
    all_to_all x1, waiting for transfers between devices, local(): lax.all_to_all(spread, 'pair', 0, 0, axis_index_groups=X_GROUPS, tiled=True)  9.82 us
    ppermute x9, waiting for transfers between devices, y_send(): return lax.ppermute(part, 'pair', moves)  8.65 us
    all_to_all x1, starting transfers between devices, local(): lax.all_to_all(spread, 'pair', 0, 0, axis_index_groups=X_GROUPS, tiled=True)  7.55 us
    all_gather x1, blocking collectives, local(): gathered = lax.all_gather(screened, 'sigma')  7.44 us
    pallas_call x1, Pallas kernels, first_streams(): pl.pallas_call(body, in_specs=[pl.BlockSpec(memory_space=pltpu.HBM)] * 3,...  6.55 us
  transfers between devices with their start and end apart: 25, of which 10 were waited for; matrix products, arithmetic and copies ran while one was open for 2% of the time, Pallas kernels for 1%

profile of v2, /device:TPU:2, one launch (start us, length us, event | category | flops | bytes accessed | tf_op | source)
XLA Modules:
  0.0 116.1 jit_solution(6714691255967166268)
XLA Ops:
  0.6 6.6 %shard_map.68 = (f32[384,256]{1,0:T(8,128)S(1)}, f32[384,256]{1,0:T(8,128)S(1)}, f32[384,256]{1,0:T(8,128)S(1)}, f32[384,256]{1,0:T(8,128)S(1)}, f32[768,256]{1,...) custom-call(bf16[2048,1536]{1,0:T(8,128)(2,1)} %pairs_ref.3, s32[2,2048]{1,0:T(2,128)} %bitcast.16, ...), custom_call_target="tpu_custom_call" | custom-call | tf_op jit(solution)/shard_map/pallas_call | solution.py:234
  7.2 4.8 %shard_map.72 = (f32[96,256]{1,0:T(8,128)}, f32[96,256]{1,0:T(8,128)}, f32[384,256]{1,0:T(8,128)}, f32[384,256]{1,0:T(8,128)}, f32[192,256]{1,0:T(8,128)}, /*index=5*/f32[192,256]{1,0:T(8,128)}, f32[192,256]{1,0:T(8,128)}) custom-call(bf16[2048,1536]{1,0:T(8,128)(2,1)} %pairs_ref.3, bf16[2048,256]{1,0:T(8,128)(2,1)S(1)} %get-tuple-element.53.scaled_ref), custom_call_target="tpu_custom_call" | custom-call | tf_op jit(solution)/shard_map/pallas_call | solution.py:283
  12.0 2.0 %collective-permute-start.15 = (f32[384,256]{1,0:T(8,128)}, f32[384,256]{1,0:T(8,128)S(1)}, u32[]{:S(2)}, u32[]{:S(2)}) collective-permute-start(f32[384,256]{1,0:T(8,128)} %get-tuple-element.56), channel_id=1, source_target_pairs={{0,16},{4,20},{8,24},{12,28},{16,32},{20,36},{24,40},{28,44},{32,4... | collective-permute-start | bytes 1179656 | tf_op jit(solution)/shard_map/ppermute | solution.py:52
  14.0 1.5 %collective-permute-start.4 = (f32[768,256]{1,0:T(8,128)S(1)}, f32[768,256]{1,0:T(8,128)S(1)}, u32[]{:S(2)}, u32[]{:S(2)}) collective-permute-start(f32[768,256]{1,0:T(8,128)S(1)} %get-tuple-element.42), channel_id=1, source_target_pairs={{0,130},{1,131},{2,128},{3,129},{4,134},{5,135},{6,132},{7,133},{8... | collective-permute-start | bytes 2359304 | tf_op jit(solution)/shard_map/ppermute | solution.py:36
  15.5 4.0 %collective-permute-start.16 = (f32[384,256]{1,0:T(8,128)}, f32[384,256]{1,0:T(8,128)S(1)}, u32[]{:S(2)}, u32[]{:S(2)}) collective-permute-start(f32[384,256]{1,0:T(8,128)} %get-tuple-element.57), channel_id=1, source_target_pairs={{0,112},{4,116},{8,120},{12,124},{16,0},{20,4},{24,8},{28,12},{32,... | collective-permute-start | bytes 1179656 | tf_op jit(solution)/shard_map/ppermute | solution.py:52
  19.6 2.4 %collective-permute-start.13 = (f32[96,256]{1,0:T(8,128)}, f32[96,256]{1,0:T(8,128)S(1)}, u32[]{:S(2)}, u32[]{:S(2)}) collective-permute-start(f32[96,256]{1,0:T(8,128)} %get-tuple-element.54), channel_id=1, source_target_pairs={{0,96},{4,100},{8,104},{12,108},{16,112},{20,116},{24,120},{28,124... | collective-permute-start | bytes 294920 | tf_op jit(solution)/shard_map/ppermute | solution.py:52
  21.9 0.5 collective-permute-start.14
  22.5 9.7 %collective-permute-done.13.low = f32[96,256]{1,0:T(8,128)S(1)} collective-permute-done((f32[96,256]{1,0:T(8,128)}, f32[96,256]{1,0:T(8,128)S(1)}, u32[]{:S(2)}, u32[]{:S(2)}) %collective-permute-start.13) | collective-permute-done | bytes 98336 | tf_op jit(solution)/shard_map/ppermute | solution.py:52
  32.2 1.6 %collective-permute-start = (f32[384,256]{1,0:T(8,128)S(1)}, f32[384,256]{1,0:T(8,128)S(1)}, u32[]{:S(2)}, u32[]{:S(2)}) collective-permute-start(f32[384,256]{1,0:T(8,128)S(1)} %get-tuple-element.36), channel_id=1, source_target_pairs={{0,4},{4,8},{8,12},{12,0},{16,20},{20,24},{24,28},{28,16},{32,36},... | collective-permute-start | bytes 1179656 | tf_op jit(solution)/shard_map/ppermute | solution.py:44
  33.8 0.0 collective-permute-done.14.high
  33.8 1.7 %collective-permute-start.1 = (f32[384,256]{1,0:T(8,128)S(1)}, f32[384,256]{1,0:T(8,128)S(1)}, u32[]{:S(2)}, u32[]{:S(2)}) collective-permute-start(f32[384,256]{1,0:T(8,128)S(1)} %get-tuple-element.37), channel_id=1, source_target_pairs={{0,12},{4,0},{8,4},{12,8},{16,28},{20,16},{24,20},{28,24},{32,44},... | collective-permute-start | bytes 1179656 | tf_op jit(solution)/shard_map/ppermute | solution.py:44
  35.4 0.0 collective-permute-done.15.up
  35.4 2.0 %collective-permute-start.2 = (f32[384,256]{1,0:T(8,128)S(1)}, f32[384,256]{1,0:T(8,128)S(1)}, u32[]{:S(2)}, u32[]{:S(2)}) collective-permute-start(f32[384,256]{1,0:T(8,128)S(1)} %get-tuple-element.38), channel_id=1, source_target_pairs={{0,8},{4,12},{8,0},{12,4},{16,24},{20,28},{24,16},{28,20},{32,40},... | collective-permute-start | bytes 1179656 | tf_op jit(solution)/shard_map/ppermute | solution.py:44
  37.4 0.0 collective-permute-done.16.down
  37.4 1.2 %shard_map.73 = (f32[192,256]{1,0:T(8,128)S(1)}, f32[192,256]{1,0:T(8,128)S(1)}, f32[192,256]{1,0:T(8,128)S(1)}) custom-call(f32[96,256]{1,0:T(8,128)S(1)} %collective-permute-done.13.low, f32[96,256]{1,0:T(8,128)S(1)} %collective-permute-done.14.high, f32[384,256]{1,0:T(8,128)S(1)} %collective-permute-done.15.up, ...), custom_call_target="tpu_custom_call" | custom-call | tf_op jit(solution)/shard_map/pallas_call | solution.py:77
  38.6 5.4 %collective-permute-start.17 = (f32[192,256]{1,0:T(8,128)S(1)}, f32[192,256]{1,0:T(8,128)S(1)}, u32[]{:S(2)}, u32[]{:S(2)}) collective-permute-start(f32[192,256]{1,0:T(8,128)S(1)} %get-tuple-element.61), channel_id=1, source_target_pairs={{0,32},{4,36},{8,40},{12,44},{16,48},{20,52},{24,56},{28,60},{32,6... | collective-permute-start | bytes 589832 | tf_op jit(solution)/shard_map/ppermute | solution.py:52
  44.0 0.3 collective-permute-done.two
  44.3 4.5 %collective-permute-start.18 = (f32[192,256]{1,0:T(8,128)S(1)}, f32[192,256]{1,0:T(8,128)S(1)}, u32[]{:S(2)}, u32[]{:S(2)}) collective-permute-start(f32[192,256]{1,0:T(8,128)S(1)} %get-tuple-element.62), channel_id=1, source_target_pairs={{0,96},{4,100},{8,104},{12,108},{16,112},{20,116},{24,120},{28,124... | collective-permute-start | bytes 589832 | tf_op jit(solution)/shard_map/ppermute | solution.py:52
  48.7 0.0 collective-permute-done.1.three
  48.7 4.0 %collective-permute-done.2.four = f32[384,256]{1,0:T(8,128)S(1)} collective-permute-done((f32[384,256]{1,0:T(8,128)S(1)}, f32[384,256]{1,0:T(8,128)S(1)}, u32[]{:S(2)}, u32[]{:S(2)}) %collective-permute-start.2) | collective-permute-done | bytes 393248 | tf_op jit(solution)/shard_map/ppermute | solution.py:44
  52.8 0.1 shard_map.69
  52.9 0.6 collective-permute-start.3
  53.5 0.0 collective-permute-done.4.other
  53.5 0.1 shard_map.70
  53.6 1.2 %collective-permute-start.5 = (f32[192,256]{1,0:T(8,128)S(1)}, f32[192,256]{1,0:T(8,128)S(1)}, u32[]{:S(2)}, u32[]{:S(2)}) collective-permute-start(f32[192,256]{1,0:T(8,128)S(1)} %get-tuple-element.44), channel_id=1, source_target_pairs={{0,4},{4,8},{8,12},{12,0},{16,20},{20,24},{24,28},{28,16},{32,36},... | collective-permute-start | bytes 589832 | tf_op jit(solution)/shard_map/ppermute | solution.py:44
  54.8 0.1 dynamic_slice.10
  54.9 2.1 %collective-permute-start.6 = (f32[192,256]{1,0:T(8,128)S(1)}, f32[192,256]{1,0:T(8,128)S(1)}, u32[]{:S(2)}, u32[]{:S(2)}) collective-permute-start(f32[192,256]{1,0:T(8,128)S(1)} %get-tuple-element.45), channel_id=1, source_target_pairs={{0,12},{4,0},{8,4},{12,8},{16,28},{20,16},{24,20},{28,24},{32,44},... | collective-permute-start | bytes 589832 | tf_op jit(solution)/shard_map/ppermute | solution.py:44
  57.0 0.0 collective-permute-done.17.above
  57.0 3.7 %collective-permute-start.7 = (f32[192,256]{1,0:T(8,128)S(1)}, f32[192,256]{1,0:T(8,128)S(1)}, u32[]{:S(2)}, u32[]{:S(2)}) collective-permute-start(f32[192,256]{1,0:T(8,128)S(1)} %get-tuple-element.46), channel_id=1, source_target_pairs={{0,8},{4,12},{8,0},{12,4},{16,24},{20,28},{24,16},{28,20},{32,40},... | collective-permute-start | bytes 589832 | tf_op jit(solution)/shard_map/ppermute | solution.py:44
  60.7 0.7 dynamic-slice_convert_fusion
  61.5 0.0 collective-permute-done.18.below
  61.5 0.8 collective-permute-start.21
  62.4 0.0 collective-permute-done.3.other
  62.4 1.4 %collective-permute-start.20 = (f32[48,256]{1,0:T(8,128)S(1)}, f32[48,256]{1,0:T(8,128)S(1)}, u32[]{:S(2)}, u32[]{:S(2)}) collective-permute-start(f32[48,256]{1,0:T(8,128)S(1)} %get-tuple-element.66), channel_id=1, source_target_pairs={{0,12},{4,0},{8,4},{12,8},{16,28},{20,16},{24,20},{28,24},{32,44},... | collective-permute-start | bytes 147464 | tf_op jit(solution)/shard_map/ppermute | solution.py:44
  63.7 0.0 collective-permute-done.5.refs_1_
  63.7 0.7 collective-permute-start.19
  64.4 1.1 collective-permute-done.7.refs_3_
  65.5 0.1 shard_map.71
  65.6 0.0 copy-start
  65.6 0.2 collective-permute-start.8
  65.8 1.4 %collective-permute-done.21 = f32[48,256]{1,0:T(8,128)S(1)} collective-permute-done((f32[48,256]{1,0:T(8,128)S(1)}, f32[48,256]{1,0:T(8,128)S(1)}, u32[]{:S(2)}, u32[]{:S(2)}) %collective-permute-start.21) | collective-permute-done | bytes 49184 | tf_op jit(solution)/shard_map/ppermute | solution.py:44
  67.2 1.8 %collective-permute-done.19 = f32[48,256]{1,0:T(8,128)S(1)} collective-permute-done((f32[48,256]{1,0:T(8,128)S(1)}, f32[48,256]{1,0:T(8,128)S(1)}, u32[]{:S(2)}, u32[]{:S(2)}) %collective-permute-start.19) | collective-permute-done | bytes 49184 | tf_op jit(solution)/shard_map/ppermute | solution.py:44
  69.1 1.6 %collective-permute-start.22 = (f32[24,256]{1,0:T(8,128)S(1)}, f32[24,256]{1,0:T(8,128)S(1)}, u32[]{:S(2)}, u32[]{:S(2)}) collective-permute-start(f32[24,256]{1,0:T(8,128)S(1)} %get-tuple-element.78), channel_id=1, source_target_pairs={{0,130},{1,131},{2,128},{3,129},{4,134},{5,135},{6,132},{7,133},{8... | collective-permute-start | bytes 73736 | tf_op jit(solution)/shard_map/ppermute | solution.py:36
  70.6 0.0 collective-permute-start.9
  70.7 3.9 %collective-permute-start.11 = (f32[48,256]{1,0:T(8,128)S(1)}, f32[48,256]{1,0:T(8,128)S(1)}, u32[]{:S(2)}, u32[]{:S(2)}) collective-permute-start(f32[48,256]{1,0:T(8,128)S(1)} %get-tuple-element.52), channel_id=1, source_target_pairs={{0,96},{4,100},{8,104},{12,108},{16,112},{20,116},{24,120},{28,124... | collective-permute-start | bytes 147464 | tf_op jit(solution)/shard_map/ppermute | solution.py:52
  74.6 0.0 collective-permute-done.8.up
  74.6 0.3 collective-permute-start.10
  74.9 3.0 %collective-permute-done.11 = f32[48,256]{1,0:T(8,128)S(1)} collective-permute-done((f32[48,256]{1,0:T(8,128)S(1)}, f32[48,256]{1,0:T(8,128)S(1)}, u32[]{:S(2)}, u32[]{:S(2)}) %collective-permute-start.11) | collective-permute-done | bytes 49184 | tf_op jit(solution)/shard_map/ppermute | solution.py:52
  77.8 3.3 %collective-permute-start.12 = (f32[48,256]{1,0:T(8,128)S(1)}, f32[48,256]{1,0:T(8,128)S(1)}, u32[]{:S(2)}, u32[]{:S(2)}) collective-permute-start(f32[48,256]{1,0:T(8,128)S(1)} %fusion.9), channel_id=1, source_target_pairs={{0,96},{4,100},{8,104},{12,108},{16,112},{20,116},{24,120},{28,124... | collective-permute-start | bytes 147464 | tf_op jit(solution)/shard_map/ppermute | solution.py:52
  81.2 0.1 negate_bitcast_fusion
  81.2 0.1 copy.13.by_row
  81.3 0.0 collective-permute-done.22.other
  81.3 0.0 collective-permute-done.10.above
  81.4 1.6 %collective-permute-done.12.below = f32[48,256]{1,0:T(8,128)S(1)} collective-permute-done((f32[48,256]{1,0:T(8,128)S(1)}, f32[48,256]{1,0:T(8,128)S(1)}, u32[]{:S(2)}, u32[]{:S(2)}) %collective-permute-start.12) | collective-permute-done | bytes 49184 | tf_op jit(solution)/shard_map/ppermute | solution.py:52
  82.9 0.1 shard_map.75
  83.1 7.4 %all_gather.3 = f32[4,24,2,384]{3,1,2,0:T(8,128)S(1)} all-gather(f32[1,24,2,384]{3,1,2,0:T(8,128)S(1)} %copy.14), channel_id=1, replica_groups=mesh['pair'=64,'sigma'=4] {'sigma'}, dimensions={0}, use_global_device_ids=true | all-gather | bytes 368640 | tf_op jit(solution)/shard_map/all_gather | solution.py:347
  90.5 0.9 multiply_reduce_fusion
  91.5 0.8 collective-permute-start.23
  92.3 4.4 %collective-permute-done.23 = f32[8,128]{1,0:T(8,128)S(1)} collective-permute-done((f32[8,128]{1,0:T(8,128)S(1)}, f32[8,128]{1,0:T(8,128)S(1)}, u32[]{:S(2)}, u32[]{:S(2)}) %collective-permute-start.23) | collective-permute-done | bytes 4128 | tf_op jit(solution)/shard_map/ppermute | solution.py:357
  96.7 0.7 broadcast_in_dim.15
  97.3 7.6 %all-to-all-start = ((f32[32,8,128]{2,1,0:T(8,128)}), f32[32,8,128]{2,1,0:T(8,128)S(1)}, u32[]{:S(2)}, u32[]{:S(2)}) async-start(f32[32,8,128]{2,1,0:T(8,128)} %broadcast_in_dim.15), calls=%async_computation | async-start | bytes 262144 | tf_op jit(solution)/shard_map/all_to_all | solution.py:359
  104.9 0.7 copy.15
  105.6 9.8 %all-to-all-done = f32[32,8,128]{2,1,0:T(8,128)S(1)} async-done(((f32[32,8,128]{2,1,0:T(8,128)}), f32[32,8,128]{2,1,0:T(8,128)S(1)}, u32[]{:S(2)}, u32[]{:S(2)}) %all-to-all-start) | async-done | bytes 131104 | tf_op jit(solution)/shard_map/all_to_all | solution.py:359
  115.5 0.6 reshape.21
  (20 shorter events, 0.2 us)
Async XLA Ops:
  12.0 23.4 %collective-permute-start.15 = (f32[384,256]{1,0:T(8,128)}, f32[384,256]{1,0:T(8,128)S(1)}, u32[]{:S(2)}, u32[]{:S(2)}) collective-permute-start(f32[384,256]{1,0:T(8,128)} %get-tuple-element.56), channel_id=1, source_target_pairs={{0,16},{4,20},{8,24},{12,28},{16,32},{20,36},{24,40},{28,44},{32,4... | collective-permute-start | bytes 1179656 | tf_op jit(solution)/shard_map/ppermute | solution.py:52
  14.0 39.5 %collective-permute-start.4 = (f32[768,256]{1,0:T(8,128)S(1)}, f32[768,256]{1,0:T(8,128)S(1)}, u32[]{:S(2)}, u32[]{:S(2)}) collective-permute-start(f32[768,256]{1,0:T(8,128)S(1)} %get-tuple-element.42), channel_id=1, source_target_pairs={{0,130},{1,131},{2,128},{3,129},{4,134},{5,135},{6,132},{7,133},{8... | collective-permute-start | bytes 2359304 | tf_op jit(solution)/shard_map/ppermute | solution.py:36
  15.5 21.9 %collective-permute-start.16 = (f32[384,256]{1,0:T(8,128)}, f32[384,256]{1,0:T(8,128)S(1)}, u32[]{:S(2)}, u32[]{:S(2)}) collective-permute-start(f32[384,256]{1,0:T(8,128)} %get-tuple-element.57), channel_id=1, source_target_pairs={{0,112},{4,116},{8,120},{12,124},{16,0},{20,4},{24,8},{28,12},{32,... | collective-permute-start | bytes 1179656 | tf_op jit(solution)/shard_map/ppermute | solution.py:52
  19.6 12.6 %collective-permute-start.13 = (f32[96,256]{1,0:T(8,128)}, f32[96,256]{1,0:T(8,128)S(1)}, u32[]{:S(2)}, u32[]{:S(2)}) collective-permute-start(f32[96,256]{1,0:T(8,128)} %get-tuple-element.54), channel_id=1, source_target_pairs={{0,96},{4,100},{8,104},{12,108},{16,112},{20,116},{24,120},{28,124... | collective-permute-start | bytes 294920 | tf_op jit(solution)/shard_map/ppermute | solution.py:52
  21.9 11.8 %collective-permute-start.14 = (f32[96,256]{1,0:T(8,128)}, f32[96,256]{1,0:T(8,128)S(1)}, u32[]{:S(2)}, u32[]{:S(2)}) collective-permute-start(f32[96,256]{1,0:T(8,128)} %get-tuple-element.55), channel_id=1, source_target_pairs={{0,32},{4,36},{8,40},{12,44},{16,48},{20,52},{24,56},{28,60},{32,6... | collective-permute-start | bytes 294920 | tf_op jit(solution)/shard_map/ppermute | solution.py:52
  32.2 12.1 %collective-permute-start = (f32[384,256]{1,0:T(8,128)S(1)}, f32[384,256]{1,0:T(8,128)S(1)}, u32[]{:S(2)}, u32[]{:S(2)}) collective-permute-start(f32[384,256]{1,0:T(8,128)S(1)} %get-tuple-element.36), channel_id=1, source_target_pairs={{0,4},{4,8},{8,12},{12,0},{16,20},{20,24},{24,28},{28,16},{32,36},... | collective-permute-start | bytes 1179656 | tf_op jit(solution)/shard_map/ppermute | solution.py:44
  33.8 15.0 %collective-permute-start.1 = (f32[384,256]{1,0:T(8,128)S(1)}, f32[384,256]{1,0:T(8,128)S(1)}, u32[]{:S(2)}, u32[]{:S(2)}) collective-permute-start(f32[384,256]{1,0:T(8,128)S(1)} %get-tuple-element.37), channel_id=1, source_target_pairs={{0,12},{4,0},{8,4},{12,8},{16,28},{20,16},{24,20},{28,24},{32,44},... | collective-permute-start | bytes 1179656 | tf_op jit(solution)/shard_map/ppermute | solution.py:44
  35.4 17.4 %collective-permute-start.2 = (f32[384,256]{1,0:T(8,128)S(1)}, f32[384,256]{1,0:T(8,128)S(1)}, u32[]{:S(2)}, u32[]{:S(2)}) collective-permute-start(f32[384,256]{1,0:T(8,128)S(1)} %get-tuple-element.38), channel_id=1, source_target_pairs={{0,8},{4,12},{8,0},{12,4},{16,24},{20,28},{24,16},{28,20},{32,40},... | collective-permute-start | bytes 1179656 | tf_op jit(solution)/shard_map/ppermute | solution.py:44
  38.6 18.4 %collective-permute-start.17 = (f32[192,256]{1,0:T(8,128)S(1)}, f32[192,256]{1,0:T(8,128)S(1)}, u32[]{:S(2)}, u32[]{:S(2)}) collective-permute-start(f32[192,256]{1,0:T(8,128)S(1)} %get-tuple-element.61), channel_id=1, source_target_pairs={{0,32},{4,36},{8,40},{12,44},{16,48},{20,52},{24,56},{28,60},{32,6... | collective-permute-start | bytes 589832 | tf_op jit(solution)/shard_map/ppermute | solution.py:52
  44.3 17.2 %collective-permute-start.18 = (f32[192,256]{1,0:T(8,128)S(1)}, f32[192,256]{1,0:T(8,128)S(1)}, u32[]{:S(2)}, u32[]{:S(2)}) collective-permute-start(f32[192,256]{1,0:T(8,128)S(1)} %get-tuple-element.62), channel_id=1, source_target_pairs={{0,96},{4,100},{8,104},{12,108},{16,112},{20,116},{24,120},{28,124... | collective-permute-start | bytes 589832 | tf_op jit(solution)/shard_map/ppermute | solution.py:52
  52.8 2.0 %copy-start.1 = (f32[1536]{0:T(1024)S(1)}, f32[1536]{0:T(1024)}, u32[]{:S(2)}) copy-start(f32[1536]{0:T(1024)} %param.8) | copy-start | bytes 18436
  52.9 9.5 %collective-permute-start.3 = (f32[192,256]{1,0:T(8,128)S(1)}, f32[192,256]{1,0:T(8,128)S(1)}, u32[]{:S(2)}, u32[]{:S(2)}) collective-permute-start(f32[192,256]{1,0:T(8,128)S(1)} %get-tuple-element.40), channel_id=1, source_target_pairs={{0,130},{1,131},{2,128},{3,129},{4,134},{5,135},{6,132},{7,133},{8... | collective-permute-start | bytes 589832 | tf_op jit(solution)/shard_map/ppermute | solution.py:36
  53.6 10.2 %collective-permute-start.5 = (f32[192,256]{1,0:T(8,128)S(1)}, f32[192,256]{1,0:T(8,128)S(1)}, u32[]{:S(2)}, u32[]{:S(2)}) collective-permute-start(f32[192,256]{1,0:T(8,128)S(1)} %get-tuple-element.44), channel_id=1, source_target_pairs={{0,4},{4,8},{8,12},{12,0},{16,20},{20,24},{24,28},{28,16},{32,36},... | collective-permute-start | bytes 589832 | tf_op jit(solution)/shard_map/ppermute | solution.py:44
  54.9 9.5 %collective-permute-start.6 = (f32[192,256]{1,0:T(8,128)S(1)}, f32[192,256]{1,0:T(8,128)S(1)}, u32[]{:S(2)}, u32[]{:S(2)}) collective-permute-start(f32[192,256]{1,0:T(8,128)S(1)} %get-tuple-element.45), channel_id=1, source_target_pairs={{0,12},{4,0},{8,4},{12,8},{16,28},{20,16},{24,20},{28,24},{32,44},... | collective-permute-start | bytes 589832 | tf_op jit(solution)/shard_map/ppermute | solution.py:44
  57.0 8.5 %collective-permute-start.7 = (f32[192,256]{1,0:T(8,128)S(1)}, f32[192,256]{1,0:T(8,128)S(1)}, u32[]{:S(2)}, u32[]{:S(2)}) collective-permute-start(f32[192,256]{1,0:T(8,128)S(1)} %get-tuple-element.46), channel_id=1, source_target_pairs={{0,8},{4,12},{8,0},{12,4},{16,24},{20,28},{24,16},{28,20},{32,40},... | collective-permute-start | bytes 589832 | tf_op jit(solution)/shard_map/ppermute | solution.py:44
  61.5 5.7 %collective-permute-start.21 = (f32[48,256]{1,0:T(8,128)S(1)}, f32[48,256]{1,0:T(8,128)S(1)}, u32[]{:S(2)}, u32[]{:S(2)}) collective-permute-start(f32[48,256]{1,0:T(8,128)S(1)} %get-tuple-element.67), channel_id=1, source_target_pairs={{0,8},{4,12},{8,0},{12,4},{16,24},{20,28},{24,16},{28,20},{32,40},... | collective-permute-start | bytes 147464 | tf_op jit(solution)/shard_map/ppermute | solution.py:44
  62.4 4.8 %collective-permute-start.20 = (f32[48,256]{1,0:T(8,128)S(1)}, f32[48,256]{1,0:T(8,128)S(1)}, u32[]{:S(2)}, u32[]{:S(2)}) collective-permute-start(f32[48,256]{1,0:T(8,128)S(1)} %get-tuple-element.66), channel_id=1, source_target_pairs={{0,12},{4,0},{8,4},{12,8},{16,28},{20,16},{24,20},{28,24},{32,44},... | collective-permute-start | bytes 147464 | tf_op jit(solution)/shard_map/ppermute | solution.py:44
  63.7 5.3 %collective-permute-start.19 = (f32[48,256]{1,0:T(8,128)S(1)}, f32[48,256]{1,0:T(8,128)S(1)}, u32[]{:S(2)}, u32[]{:S(2)}) collective-permute-start(f32[48,256]{1,0:T(8,128)S(1)} %get-tuple-element.65), channel_id=1, source_target_pairs={{0,4},{4,8},{8,12},{12,0},{16,20},{20,24},{24,28},{28,16},{32,36},... | collective-permute-start | bytes 147464 | tf_op jit(solution)/shard_map/ppermute | solution.py:44
  65.6 25.0 %copy-start = (bf16[1536,512]{1,0:T(8,128)(2,1)S(1)}, bf16[1536,512]{1,0:T(8,128)(2,1)}, u32[]{:S(2)}) copy-start(bf16[1536,512]{1,0:T(8,128)(2,1)} %param.9) | copy-start | bytes 4718596
  65.6 9.0 %collective-permute-start.8 = (f32[96,256]{1,0:T(8,128)S(1)}, f32[96,256]{1,0:T(8,128)S(1)}, u32[]{:S(2)}, u32[]{:S(2)}) collective-permute-start(f32[96,256]{1,0:T(8,128)S(1)} %get-tuple-element.48), channel_id=1, source_target_pairs={{0,16},{4,20},{8,24},{12,28},{16,32},{20,36},{24,40},{28,44},{32,4... | collective-permute-start | bytes 294920 | tf_op jit(solution)/shard_map/ppermute | solution.py:52
  69.1 12.3 %collective-permute-start.22 = (f32[24,256]{1,0:T(8,128)S(1)}, f32[24,256]{1,0:T(8,128)S(1)}, u32[]{:S(2)}, u32[]{:S(2)}) collective-permute-start(f32[24,256]{1,0:T(8,128)S(1)} %get-tuple-element.78), channel_id=1, source_target_pairs={{0,130},{1,131},{2,128},{3,129},{4,134},{5,135},{6,132},{7,133},{8... | collective-permute-start | bytes 73736 | tf_op jit(solution)/shard_map/ppermute | solution.py:36
  70.6 7.2 %collective-permute-start.9 = (f32[96,256]{1,0:T(8,128)S(1)}, f32[96,256]{1,0:T(8,128)S(1)}, u32[]{:S(2)}, u32[]{:S(2)}) collective-permute-start(f32[96,256]{1,0:T(8,128)S(1)} %get-tuple-element.49), channel_id=1, source_target_pairs={{0,112},{4,116},{8,120},{12,124},{16,0},{20,4},{24,8},{28,12},{32,... | collective-permute-start | bytes 294920 | tf_op jit(solution)/shard_map/ppermute | solution.py:52
  70.7 7.2 %collective-permute-start.11 = (f32[48,256]{1,0:T(8,128)S(1)}, f32[48,256]{1,0:T(8,128)S(1)}, u32[]{:S(2)}, u32[]{:S(2)}) collective-permute-start(f32[48,256]{1,0:T(8,128)S(1)} %get-tuple-element.52), channel_id=1, source_target_pairs={{0,96},{4,100},{8,104},{12,108},{16,112},{20,116},{24,120},{28,124... | collective-permute-start | bytes 147464 | tf_op jit(solution)/shard_map/ppermute | solution.py:52
  74.6 6.7 %collective-permute-start.10 = (f32[48,256]{1,0:T(8,128)S(1)}, f32[48,256]{1,0:T(8,128)S(1)}, u32[]{:S(2)}, u32[]{:S(2)}) collective-permute-start(f32[48,256]{1,0:T(8,128)S(1)} %slice_add_fusion.1), channel_id=1, source_target_pairs={{0,32},{4,36},{8,40},{12,44},{16,48},{20,52},{24,56},{28,60},{32,6... | collective-permute-start | bytes 147464 | tf_op jit(solution)/shard_map/ppermute | solution.py:52
  77.8 5.1 %collective-permute-start.12 = (f32[48,256]{1,0:T(8,128)S(1)}, f32[48,256]{1,0:T(8,128)S(1)}, u32[]{:S(2)}, u32[]{:S(2)}) collective-permute-start(f32[48,256]{1,0:T(8,128)S(1)} %fusion.9), channel_id=1, source_target_pairs={{0,96},{4,100},{8,104},{12,108},{16,112},{20,116},{24,120},{28,124... | collective-permute-start | bytes 147464 | tf_op jit(solution)/shard_map/ppermute | solution.py:52
  91.5 5.2 %collective-permute-start.23 = (f32[8,128]{1,0:T(8,128)S(1)}, f32[8,128]{1,0:T(8,128)S(1)}, u32[]{:S(2)}, u32[]{:S(2)}) collective-permute-start(f32[8,128]{1,0:T(8,128)S(1)} %div.21), channel_id=1, source_target_pairs={{0,128},{4,132},{8,136},{12,140},{16,144},{20,148},{24,152},{28,15... | collective-permute-start | bytes 12296 | tf_op jit(solution)/shard_map/ppermute | solution.py:357
  97.3 18.1 %all-to-all-start = ((f32[32,8,128]{2,1,0:T(8,128)}), f32[32,8,128]{2,1,0:T(8,128)S(1)}, u32[]{:S(2)}, u32[]{:S(2)}) async-start(f32[32,8,128]{2,1,0:T(8,128)} %broadcast_in_dim.15), calls=%async_computation | async-start | bytes 262144 | tf_op jit(solution)/shard_map/all_to_all | solution.py:359
